TPU v7x, 32 devices: a whole 2x2x4 slice. The times are simulated.
32 devices in a mesh: fsdp: 8 (over z, x), head: 2 (over core), tensor: 2 (over y).
Axes of the slice: x: 2, y: 2, z: 4, core: 2. Of those that a mesh axis runs over, the one named last changes fastest.
Arguments:
- block_in: bfloat16 [4096, 1024], P('fsdp'), may hold values from -6 to 6
- cotangent: bfloat16 [4096, 1024], P('fsdp'), may hold values from -6 to 6
- norm_gain: float32 [1024], replicated, may hold values from 0.5 to 1.5
- w_x: bfloat16 [1024, 32, 64], P('fsdp', 'head', 'tensor'), may hold values from -0.1875 to 0.1875
- w_z: bfloat16 [1024, 32, 64], P('fsdp', 'head', 'tensor'), may hold values from -0.1875 to 0.1875
- w_bc: bfloat16 [1024, 2, 128], P('fsdp'), may hold values from -0.1875 to 0.1875
- w_dt: bfloat16 [1024, 32], P('fsdp', 'head'), may hold values from -0.1875 to 0.1875
- conv_x: float32 [32, 64, 4], P('head', 'tensor'), may hold values from -3 to 3
- conv_bc: float32 [2, 128, 4], replicated, may hold values from -3 to 3
- dt_bias: float32 [32], P('head'), may hold values from -6 to -2
- a_log: float32 [32], P('head'), may hold values from -1.5 to 0.5
- skip: float32 [32], P('head'), may hold values from 0.5 to 1.5
- gate_gain: float32 [32, 64], P('head', 'tensor'), may hold values from 0.5 to 1.5
- w_out: bfloat16 [32, 64, 1024], P('head', 'tensor', 'fsdp'), may hold values from -0.125 to 0.125
Outputs:
- block_out: bfloat16 [4096, 1024], P('fsdp')
- grad_in: float32 [4096, 1024], P('fsdp')
- grad_norm_gain: float32 [1024], replicated
- grad_w_x: float32 [1024, 32, 64], P('fsdp', 'head', 'tensor')
- grad_w_z: float32 [1024, 32, 64], P('fsdp', 'head', 'tensor')
- grad_w_bc: float32 [1024, 2, 128], P('fsdp')
- grad_w_dt: float32 [1024, 32], P('fsdp', 'head')
- grad_conv_x: float32 [32, 64, 4], P('head', 'tensor')
- grad_conv_bc: float32 [2, 128, 4], replicated
- grad_dt_bias: float32 [32], P('head')
- grad_a_log: float32 [32], P('head')
- grad_skip: float32 [32], P('head')
- grad_gate_gain: float32 [32, 64], P('head', 'tensor')
- grad_w_out: float32 [32, 64, 1024], P('head', 'tensor', 'fsdp')
All inputs are finite; a program needn't handle non-finite values.
Results may differ from a plain program's by a relative error of at most 0.011.
Values may be sent and summed in bfloat16 or wider, within the bound.
A program may use at most 128 MiB of HBM per device.

v0:
```python
from functools import partial

import jax
import jax.numpy as jnp
from jax import lax
from jax.sharding import PartitionSpec as P

SPAN = 256


EPSILON = 1e-05
PRECISE = lax.Precision.HIGHEST


def causal_conv(signal, kernel):
    taps = kernel.shape[1]
    length = signal.shape[0]
    padded = jnp.pad(signal, ((taps - 1, 0), (0, 0)))
    total = jnp.zeros_like(signal)
    for offset in range(taps):
        total = total + padded[offset : offset + length] * kernel[:, offset]
    return total


def conv_silu(signal, kernel):
    return jax.nn.silu(causal_conv(signal, kernel))


def silu_slope(value):
    sigma = jax.nn.sigmoid(value)
    return sigma * (1.0 + value * (1.0 - sigma))


def scan_spans(values, step_size, rate, b_maps, c_maps, block):
    length, head_count, channels = values.shape
    blocks = length // block
    logs = (step_size * rate).reshape(blocks, block, head_count)
    cums = jnp.cumsum(logs, axis=1)
    x_blocks = values.reshape(blocks, block, head_count, channels)
    dt_blocks = step_size.reshape(blocks, block, head_count)
    b_blocks = b_maps.reshape(blocks, block, -1)
    c_blocks = c_maps.reshape(blocks, block, -1)
    scores = jnp.einsum("cln,csn->cls", c_blocks, b_blocks, precision=PRECISE)
    causal = (jnp.arange(block)[:, None] >= jnp.arange(block)[None, :])[None, :, :, None]
    gaps = cums[:, :, None, :] - cums[:, None, :, :]
    decays = jnp.where(causal, jnp.exp(jnp.where(causal, gaps, 0.0)), 0.0)
    mixing = scores[..., None] * decays * dt_blocks[:, None, :, :]
    intra_part = jnp.einsum("clsh,cshp->clhp", mixing, x_blocks, precision=PRECISE)
    to_end = jnp.exp(cums[:, -1:, :] - cums) * dt_blocks
    states = jnp.einsum("csh,csn,cshp->chpn", to_end, b_blocks, x_blocks, precision=PRECISE)
    whole_decay = jnp.exp(cums[:, -1, :])
    carried = []
    running = jnp.zeros_like(states[0])
    for position in range(blocks):
        carried.append(running)
        running = running * whole_decay[position][:, None, None] + states[position]
    entering = jnp.stack(carried)
    inter_part = jnp.einsum(
        "cln,clh,chpn->clhp", c_blocks, jnp.exp(cums), entering, precision=PRECISE
    )
    return (intra_part + inter_part).reshape(length, head_count, channels)


def mixer(values, dt_raw, dt_bias, a_log, skip, b_maps, c_maps, block):
    step_size = jax.nn.softplus(dt_raw + dt_bias)
    rate = -jnp.exp(a_log)
    return scan_spans(values, step_size, rate, b_maps, c_maps, block) + skip[:, None] * values


def on_device(
    block_in,
    cotangent,
    norm_gain,
    w_x,
    w_z,
    w_bc,
    w_dt,
    conv_x,
    conv_bc,
    dt_bias,
    a_log,
    skip,
    gate_gain,
    w_out,
):
    length, model_width = block_in.shape
    head_count, head_width, taps = conv_x.shape
    state_size = conv_bc.shape[1]
    inner_width = head_count * head_width
    group_count = lax.axis_size("head") * lax.axis_size("tensor")
    full_inner = inner_width * group_count
    weights = (w_x, w_z, w_bc, w_dt, w_out)
    gathered = (
        lax.all_gather(weights[0], "fsdp", axis=0, tiled=True),
        lax.all_gather(weights[1], "fsdp", axis=0, tiled=True),
        lax.all_gather(weights[2], "fsdp", axis=0, tiled=True),
        lax.all_gather(weights[3], "fsdp", axis=0, tiled=True),
        lax.all_gather(weights[4], "fsdp", axis=2, tiled=True),
    )
    weight_x = gathered[0].reshape(model_width, inner_width)
    weight_z = gathered[1].reshape(model_width, inner_width)
    weight_bc = gathered[2].reshape(model_width, 2 * state_size)
    weight_dt = gathered[3]
    weight_out = gathered[4].reshape(inner_width, model_width)
    kernel_x = conv_x.reshape(inner_width, taps)
    kernel_bc = conv_bc.reshape(2 * state_size, taps)
    gain_flat = gate_gain.reshape(inner_width)
    features = block_in.astype(jnp.float32)
    scale_in = lax.rsqrt(jnp.mean(features * features, axis=1, keepdims=True) + EPSILON)
    normed = (features * scale_in * norm_gain).astype(jnp.bfloat16)
    x_raw = jnp.dot(normed, weight_x, preferred_element_type=jnp.float32)
    z_raw = jnp.dot(normed, weight_z, preferred_element_type=jnp.float32)
    bc_raw = jnp.dot(normed, weight_bc, preferred_element_type=jnp.float32)
    dt_raw = jnp.dot(normed, weight_dt, preferred_element_type=jnp.float32)
    x_act = conv_silu(x_raw, kernel_x).astype(jnp.bfloat16)
    bc_act = conv_silu(bc_raw, kernel_bc).astype(jnp.bfloat16)
    values = x_act.astype(jnp.float32).reshape(length, head_count, head_width)
    b_maps = bc_act[:, :state_size].astype(jnp.float32)
    c_maps = bc_act[:, state_size:].astype(jnp.float32)
    mixed = mixer(values, dt_raw, dt_bias, a_log, skip, b_maps, c_maps, SPAN).reshape(
        length, inner_width
    )
    gated = mixed * jax.nn.silu(z_raw)
    square_sum = lax.psum(jnp.sum(gated * gated, axis=1), ("head", "tensor"))
    scale_out = lax.rsqrt(square_sum / full_inner + EPSILON)[:, None]
    normed_out = (gated * scale_out * gain_flat).astype(jnp.bfloat16)
    partial_out = jnp.dot(normed_out, weight_out, preferred_element_type=jnp.float32)
    summed = lax.psum(partial_out, ("head", "tensor"))
    block_out = (summed + features).astype(jnp.bfloat16)
    again = (
        lax.all_gather(weights[0], "fsdp", axis=0, tiled=True),
        lax.all_gather(weights[1], "fsdp", axis=0, tiled=True),
        lax.all_gather(weights[2], "fsdp", axis=0, tiled=True),
        lax.all_gather(weights[3], "fsdp", axis=0, tiled=True),
        lax.all_gather(weights[4], "fsdp", axis=2, tiled=True),
    )
    back_x = again[0].reshape(model_width, inner_width)
    back_z = again[1].reshape(model_width, inner_width)
    back_bc = again[2].reshape(model_width, 2 * state_size)
    back_dt = again[3]
    back_out = again[4].reshape(inner_width, model_width)
    upstream = cotangent.astype(jnp.float32)
    d_normed_out = jnp.dot(cotangent, back_out.T, preferred_element_type=jnp.float32)
    g_w_out = jnp.dot(normed_out.T, cotangent, preferred_element_type=jnp.float32)
    g_gate_gain = jnp.sum(d_normed_out * gated * scale_out, axis=0)
    d_hat = d_normed_out * gain_flat
    inner_sum = lax.psum(jnp.sum(d_hat * gated, axis=1), ("head", "tensor"))[:, None]
    d_gated = scale_out * d_hat - gated * scale_out**3 * inner_sum / full_inner
    d_mixed = d_gated * jax.nn.silu(z_raw)
    d_z = (d_gated * mixed * silu_slope(z_raw)).astype(jnp.bfloat16)
    _, pullback = jax.vjp(
        partial(mixer, block=SPAN), values, dt_raw, dt_bias, a_log, skip, b_maps, c_maps
    )
    d_xs, d_dt, g_dt_bias, g_a_log, g_skip, d_b, d_c = pullback(
        d_mixed.reshape(length, head_count, head_width)
    )
    d_dt, g_dt_bias, g_a_log, g_skip = lax.psum((d_dt, g_dt_bias, g_a_log, g_skip), "tensor")
    d_bc = lax.psum(jnp.concatenate([d_b, d_c], axis=1), ("head", "tensor"))
    _, pull_x = jax.vjp(conv_silu, x_raw, kernel_x)
    d_x_raw, g_conv_x = pull_x(d_xs.reshape(length, inner_width))
    _, pull_bc = jax.vjp(conv_silu, bc_raw, kernel_bc)
    d_bc_raw, g_conv_bc = pull_bc(d_bc)
    d_x_b = d_x_raw.astype(jnp.bfloat16)
    d_bc_b = d_bc_raw.astype(jnp.bfloat16)
    d_dt_b = d_dt.astype(jnp.bfloat16)
    g_w_x = jnp.dot(normed.T, d_x_b, preferred_element_type=jnp.float32)
    g_w_z = jnp.dot(normed.T, d_z, preferred_element_type=jnp.float32)
    g_w_bc = jnp.dot(normed.T, d_bc_b, preferred_element_type=jnp.float32)
    g_w_dt = jnp.dot(normed.T, d_dt_b, preferred_element_type=jnp.float32)
    local_part = (
        jnp.dot(d_x_b, back_x.T, preferred_element_type=jnp.float32)
        + jnp.dot(d_z, back_z.T, preferred_element_type=jnp.float32)
        + jnp.dot(d_dt_b, back_dt.T, preferred_element_type=jnp.float32)
        * (1.0 / lax.axis_size("tensor"))
    )
    d_normed = lax.psum(local_part, ("head", "tensor")) + jnp.dot(
        d_bc_b, back_bc.T, preferred_element_type=jnp.float32
    )
    g_norm_gain = jnp.sum(d_normed * features * scale_in, axis=0)
    d_in_hat = d_normed * norm_gain
    grad_in = (
        scale_in * d_in_hat
        - features * scale_in**3 * jnp.mean(d_in_hat * features, axis=1, keepdims=True)
        + upstream
    )
    big_grads = (
        lax.psum_scatter(
            g_w_x.reshape(model_width, head_count, head_width),
            "fsdp",
            scatter_dimension=0,
            tiled=True,
        ),
        lax.psum_scatter(
            g_w_z.reshape(model_width, head_count, head_width),
            "fsdp",
            scatter_dimension=0,
            tiled=True,
        ),
        lax.psum_scatter(g_w_bc, "fsdp", scatter_dimension=0, tiled=True),
        lax.psum_scatter(g_w_dt, "fsdp", scatter_dimension=0, tiled=True),
        lax.psum_scatter(
            g_w_out.reshape(head_count, head_width, model_width),
            "fsdp",
            scatter_dimension=2,
            tiled=True,
        ),
    )
    owned_bc = big_grads[2].reshape(-1, 2, state_size)
    small = lax.psum(
        (
            g_norm_gain,
            g_conv_x.reshape(head_count, head_width, taps),
            g_conv_bc.reshape(2, state_size, taps),
            g_dt_bias,
            g_a_log,
            g_skip,
            g_gate_gain.reshape(head_count, head_width),
        ),
        "fsdp",
    )
    return (
        block_out,
        grad_in,
        small[0],
        big_grads[0],
        big_grads[1],
        owned_bc,
        big_grads[3],
        small[1],
        small[2],
        small[3],
        small[4],
        small[5],
        small[6],
        big_grads[4],
    )


def solution(mesh):
    return jax.shard_map(
        on_device,
        mesh=mesh,
        in_specs=(
            P("fsdp", None),
            P("fsdp", None),
            P(),
            P("fsdp", "head", "tensor"),
            P("fsdp", "head", "tensor"),
            P("fsdp", None, None),
            P("fsdp", "head"),
            P("head", "tensor", None),
            P(),
            P("head"),
            P("head"),
            P("head"),
            P("head", "tensor"),
            P("head", "tensor", "fsdp"),
        ),
        out_specs=(
            P("fsdp", None),
            P("fsdp", None),
            P(),
            P("fsdp", "head", "tensor"),
            P("fsdp", "head", "tensor"),
            P("fsdp", None, None),
            P("fsdp", "head"),
            P("head", "tensor", None),
            P(),
            P("head"),
            P("head"),
            P("head"),
            P("head", "tensor"),
            P("head", "tensor", "fsdp"),
        ),
        check_vma=False,
    )
```

profile of v0, /device:TPU:0, one launch (start us, length us, event | category | flops | bytes accessed | tf_op | source)
XLA Modules:
  0.0 669.5 jit_solution(9409954152697508148)
XLA Ops:
  13.0 28.3 %all_gather.22 = bf16[1024,16]{0,1:T(8,128)(2,1)S(1)} all-gather(bf16[128,16]{0,1:T(8,128)(2,1)} %param.20), channel_id=1, replica_groups=mesh['fsdp'=8,'head'=2,'tensor'=2] {'fsdp'}, dimensions={0}, use_global_device_ids=true | all-gather | bytes 36864 | tf_op jit(solution)/shard_map/all_gather | solution.py:97
  41.3 2.3 broadcast_multiply_fusion.8
  48.1 32.0 %all_gather.21 = bf16[1024,2,128]{2,1,0:T(2,128)(2,1)S(1)} all-gather(bf16[128,2,128]{2,1,0:T(2,128)(2,1)S(1)} %copy-done.27), channel_id=1, replica_groups=mesh['fsdp'=8,'head'=2,'tensor'=2] {'fsdp'}, dimensions={0}, use_global_device_ids=true | all-gather | bytes 589824 | tf_op jit(solution)/shard_map/all_gather | solution.py:96
  90.0 6.3 fusion.38
  98.5 3.5 multiply_reduce_fusion.9
  102.1 7.4 %psum.112 = f32[512]{0:T(512)S(1)} all-reduce(f32[512]{0:T(512)S(1)} %get-tuple-element.106), channel_id=1, replica_groups=mesh['fsdp'=8,'head'=2,'tensor'=2] {'head','tensor'}, use_global_device_ids=true, to_apply=%region_4.5 | all-reduce | flops 512 | bytes 4096 | tf_op jit(solution)/shard_map/psum | solution.py:124
  109.5 26.0 %all-gather.8.cloned.1.call-done = bf16[16,32,1024]{2,1,0:T(8,128)(2,1)} async-done(((bf16[16,32,128]{2,1,0:T(8,128)(2,1)}), bf16[16,32,1024]{2,1,0:T(8,128)(2,1)}) %all-gather.8.cloned.1.call-update) | async-done | bytes 1048592 | tf_op jit(solution)/shard_map/all_gather | solution.py:98
  135.5 3.9 multiply_reduce_fusion.3
  139.4 7.5 %psum.114 = f32[512]{0:T(512)S(1)} all-reduce(f32[512]{0:T(512)S(1)} %get-tuple-element.77), channel_id=1, replica_groups=mesh['fsdp'=8,'head'=2,'tensor'=2] {'head','tensor'}, use_global_device_ids=true, to_apply=%region_7.8 | all-reduce | flops 512 | bytes 4096 | tf_op jit(solution)/shard_map/psum | solution.py:147
  146.9 4.2 fusion.45
  152.5 2.9 reshape_reshape.8
  157.3 2.6 convolution_bitcast_fusion.1
  160.8 2.6 convolution_bitcast_fusion.2
  164.0 11.4 %fusion.9 = (f32[2,256,16]{1,2,0:T(8,128)}, f32[2,256,16]{1,2,0:T(8,128)}, f32[2,256,16]{1,2,0:T(8,128)}, f32[2,256,256]{2,1,0:T(8,128)}) fusion(f32[2,256,16]{1,2,0:T(8,128)S(1)} %bitcast.241, f32[2,256,16]{1,2,0:T(8,128)S(1)} %copy-done.26, f32[2,256,256]{2,1,0:T(8,128)S(1)} %copy-done.20, pred[256,256]{1,0:T(8,128)(4,1)S(1)} %copy-done.29, ...), kind=kOutput, calls=%fused_computation.18 | convolution fusion | flops 836608000 | bytes 2850816 | tf_op jit(solution)/shard_map/transpose(jvp(clsh,cshp->clhp))/dot_general | solution.py:48
  175.5 8.1 %fusion.41 = f32[2,256,16,32]{1,3,2,0:T(8,128)} fusion(f32[2,256,16]{1,2,0:T(8,128)S(1)} %bitcast.242, f32[2,256,16]{1,2,0:T(8,128)S(1)} %copy-done.26, f32[2,256,256]{2,1,0:T(8,128)S(1)} %copy-done.20, pred[256,256]{1,0:T(8,128)(4,1)S(1)} %copy-done.29, f32[2,256,16,32]{1,3,2,0:T(8,128)S(1)} %fusion.58, f32[2,16,32,256]{3,0,2,1:T(2,128)S(1)} %bitcast.207, ...), kind=kOutput, calls=%fused_computation.48 | convolution fusion | flops 816316416 | bytes 3833856 | tf_op jit(solution)/shard_map/transpose(jvp(clsh,cshp->clhp))/dot_general | solution.py:48
  190.2 2.5 convolution_add_fusion.2
  196.9 2.6 copy.141
  199.9 5.0 reduce-window.16
  205.4 3.6 fusion.118
  214.7 8.3 %all-reduce.25 = (bf16[512,16]{0,1:T(8,128)(2,1)S(1)}, f32[16]{0:T(128)S(1)}, f32[16]{0:T(128)S(1)}, f32[16]{0:T(128)S(1)}) all-reduce(f32[512,16]{0,1:T(8,128)S(1)} %get-tuple-element.105, f32[16]{0:T(128)S(1)} %get-tuple-element.104, f32[16]{0:T(128)S(1)} %negate_multiply_fusion, ...), channel_id=1, replica_groups=mesh['fsdp'=8,'head'=2,'tensor'=2] {'tensor'}, use_global_device_ids=true, to_apply=%region_15.16 | all-reduce | flops 8240 | bytes 49536 | tf_op jit(solution)/shard_map/psum | solution.py:157
  222.9 4.0 multiply_add_fusion
  227.0 92.5 %all-reduce.28.cloned.1.call-done = (f32[512,1024]{1,0:T(8,128)}, f32[512,1024]{1,0:T(8,128)}, f32[512,256]{1,0:T(8,128)}) async-done(((f32[512,1024]{1,0:T(8,128)}, f32[512,1024]{1,0:T(8,128)}, f32[512,256]{1,0:T(8,128)}), (f32[512,1024]{1,0:T(8,128)}, f32[512,1024]{1,0:T(8,128)}, f32[512,256]{1,0:T(8,128)})) %all-reduce.28.cloned.1.call-update) | async-done | bytes 4718608 | tf_op jit(solution)/shard_map/psum | solution.py:128
  324.8 3.4 fusion.92
  329.2 2.2 fusion.97
  333.9 2.6 fusion.31
  336.6 38.1 %all-reduce.23 = (f32[1024]{0:T(1024)}, f32[16,32,4]{1,0,2:T(8,128)S(1)}, f32[2,128,4]{1,2,0:T(4,128)}, f32[16]{0:T(128)}, f32[16]{0:T(128)}, /*index=5*/f32[16]{0:T(128)}, f32[16,32]{1,0:T(8,128)}) all-reduce(f32[1024]{0:T(1024)S(1)} %get-tuple-element.74, ...), channel_id=1, replica_groups=mesh['fsdp'=8,'head'=2,'tensor'=2] {'fsdp'}, use_global_device_ids=true, to_apply=%region_21.22 | all-reduce | flops 4656 | bytes 37248 | tf_op jit(solution)/shard_map/psum | solution.py:209
  375.3 4.3 fusion.28
  379.6 8.6 %reduce-scatter.10.cloned.1.call-done = f32[128,256]{1,0:T(8,128)} async-done(((f32[1024,256]{1,0:T(8,128)}), f32[128,256]{1,0:T(8,128)}) %reduce-scatter.10.cloned.1.call-update) | async-done | bytes 131088 | tf_op jit(solution)/shard_map/reduce_scatter | solution.py:199
  389.9 55.8 %reduce-scatter.12.cloned.1.call-done = f32[128,16]{0,1:T(8,128)} async-done(((f32[1024,16]{0,1:T(8,128)}), f32[128,16]{0,1:T(8,128)}) %reduce-scatter.12.cloned.1.call-update) | async-done | bytes 8208 | tf_op jit(solution)/shard_map/reduce_scatter | solution.py:200
  445.7 72.3 %reduce-scatter.14.cloned.1.call-done = f32[16,32,128]{2,1,0:T(8,128)} async-done(((f32[16,32,1024]{2,1,0:T(8,128)}), f32[16,32,128]{2,1,0:T(8,128)}) %reduce-scatter.14.cloned.1.call-update) | async-done | bytes 262160 | tf_op jit(solution)/shard_map/reduce_scatter | solution.py:201
  518.0 72.2 %reduce-scatter.8.cloned.1.call-done = f32[128,16,32]{0,2,1:T(8,128)} async-done(((f32[1024,16,32]{0,2,1:T(8,128)}), f32[128,16,32]{0,2,1:T(8,128)}) %reduce-scatter.8.cloned.1.call-update) | async-done | bytes 262160 | tf_op jit(solution)/shard_map/reduce_scatter | solution.py:193
  590.2 72.4 %reduce-scatter.6.cloned.1.call-done = f32[128,16,32]{0,2,1:T(8,128)} async-done(((f32[1024,16,32]{0,2,1:T(8,128)}), f32[128,16,32]{0,2,1:T(8,128)}) %reduce-scatter.6.cloned.1.call-update) | async-done | bytes 262160 | tf_op jit(solution)/shard_map/reduce_scatter | solution.py:187
  (253 shorter events, 54.8 us)
Async XLA Ops:
  7.2 39.4 %copy-start.69 = (f32[16,32]{1,0:T(8,128)S(1)}, f32[16,32]{1,0:T(8,128)}, u32[]{:S(2)}) copy-start(f32[16,32]{1,0:T(8,128)} %param.26) | copy-start | bytes 6148
  7.2 39.5 %copy-start.70 = (f32[2,128,4]{1,2,0:T(4,128)S(1)}, f32[2,128,4]{1,2,0:T(4,128)}, u32[]{:S(2)}) copy-start(f32[2,128,4]{1,2,0:T(4,128)} %param.22) | copy-start | bytes 12292
  7.2 39.5 %copy-start.75 = (f32[16]{0:T(128)S(1)}, f32[16]{0:T(128)}, u32[]{:S(2)}) copy-start(f32[16]{0:T(128)} %param.25) | copy-start | bytes 196
  7.2 40.2 %copy-start.45 = (f32[16,32,4]{1,2,0:T(4,128)S(1)}, f32[16,32,4]{1,2,0:T(4,128)}, u32[]{:S(2)}) copy-start(f32[16,32,4]{1,2,0:T(4,128)} %param.21) | copy-start | bytes 24580
  7.2 40.9 %copy-start.27 = (bf16[128,2,128]{2,1,0:T(2,128)(2,1)S(1)}, bf16[128,2,128]{2,1,0:T(2,128)(2,1)}, u32[]{:S(2)}) copy-start(bf16[128,2,128]{2,1,0:T(2,128)(2,1)} %param.19) | copy-start | bytes 196612
  7.2 75.6 %all-gather.4.cloned.1.call-start = ((), (), s32[]{:S(2)}) async-start(), calls=%async_computation.5 | async-start | bytes 1179648 | tf_op jit(solution)/shard_map/all_gather | solution.py:94
  8.0 90.6 %all-gather.6.cloned.1.call-start = ((), (), s32[]{:S(2)}) async-start(), calls=%async_computation.6 | async-start | bytes 1179648 | tf_op jit(solution)/shard_map/all_gather | solution.py:95
  8.7 126.8 %all-gather.8.cloned.1.call-start = ((), (), s32[]{:S(2)}) async-start(), calls=%async_computation.7 | async-start | bytes 1179648 | tf_op jit(solution)/shard_map/all_gather | solution.py:98
  9.4 310.1 %all-reduce.28.cloned.1.call-start = ((), (), s32[]{:S(2)}) async-start(), calls=%async_computation.13 | async-start | bytes 9437184 | tf_op jit(solution)/shard_map/psum | solution.py:128
  10.8 70.1 %copy-start = (bf16[512,1024]{1,0:T(8,128)(2,1)S(1)}, bf16[512,1024]{1,0:T(8,128)(2,1)}, u32[]{:S(2)}) copy-start(bf16[512,1024]{1,0:T(8,128)(2,1)} %param.14) | copy-start | bytes 3145732
  10.8 70.1 %copy-start.30 = (f32[1024]{0:T(1024)S(1)}, f32[1024]{0:T(1024)}, u32[]{:S(2)}) copy-start(f32[1024]{0:T(1024)} %param.16) | copy-start | bytes 12292
  13.0 85.6 %copy-start.32 = (f32[512]{0:T(512)}, f32[512]{0:T(512)S(1)}, u32[]{:S(2)}) copy-start(f32[512]{0:T(512)S(1)} %get-tuple-element.141) | copy-start | bytes 6148
  45.0 37.6 %copy-start.34 = (f32[2,16,2]{1,2,0:T(2,128)}, f32[2,16,2]{1,2,0:T(2,128)S(1)}, u32[]{:S(2)}) copy-start(f32[2,16,2]{1,2,0:T(2,128)S(1)} %slice.130) | copy-start | bytes 772
  45.0 44.9 %copy-start.25 = (f32[2,256,16]{1,2,0:T(8,128)}, f32[2,256,16]{1,2,0:T(8,128)S(1)}, u32[]{:S(2)}) copy-start(f32[2,256,16]{1,2,0:T(8,128)S(1)} %bitcast_bitcast_fusion.1) | copy-start | bytes 98308
  45.2 143.0 %copy-start.36 = (f32[2,16]{1,0:T(2,128)}, f32[2,16]{1,0:T(2,128)S(1)}, u32[]{:S(2)}) copy-start(f32[2,16]{1,0:T(2,128)S(1)} %slice_reduce_fusion.2) | copy-start | bytes 388
  46.6 137.8 %copy-start.38 = (f32[512]{0:T(512)}, f32[512]{0:T(512)S(1)}, u32[]{:S(2)}) copy-start(f32[512]{0:T(512)S(1)} %mul.547) | copy-start | bytes 6148
  47.5 37.5 %copy-start.50 = (f32[512,1]{0,1:T(1,128)}, f32[512,1]{0,1:T(1,128)S(1)}, u32[]{:S(2)}) copy-start(f32[512,1]{0,1:T(1,128)S(1)} %get-tuple-element.132) | copy-start | bytes 6148
  47.6 37.5 %copy-start.52 = (f32[512,1]{0,1:T(1,128)}, f32[512,1]{0,1:T(1,128)S(1)}, u32[]{:S(2)}) copy-start(f32[512,1]{0,1:T(1,128)S(1)} %get-tuple-element.133) | copy-start | bytes 6148
  47.6 37.5 %copy-start.54 = (f32[512,1]{0,1:T(1,128)}, f32[512,1]{0,1:T(1,128)S(1)}, u32[]{:S(2)}) copy-start(f32[512,1]{0,1:T(1,128)S(1)} %get-tuple-element.134) | copy-start | bytes 6148
  47.6 37.5 %copy-start.56 = (f32[512,1]{0,1:T(1,128)}, f32[512,1]{0,1:T(1,128)S(1)}, u32[]{:S(2)}) copy-start(f32[512,1]{0,1:T(1,128)S(1)} %get-tuple-element.135) | copy-start | bytes 6148
  109.5 74.9 %copy-start.40 = (f32[512]{0:T(512)}, f32[512]{0:T(512)S(1)}, u32[]{:S(2)}) copy-start(f32[512]{0:T(512)S(1)} %get-tuple-element.143) | copy-start | bytes 6148
  226.9 92.7 %copy-start.13 = (f32[512,256]{1,0:T(8,128)S(1)}, f32[512,256]{1,0:T(8,128)}, u32[]{:S(2)}) copy-start(f32[512,256]{1,0:T(8,128)} %copy-done.12) | copy-start | bytes 1572868
  226.9 94.3 %copy-start.61 = (f32[256,1]{0,1:T(1,128)S(1)}, f32[256,1]{0,1:T(1,128)}, u32[]{:S(2)}) copy-start(f32[256,1]{0,1:T(1,128)} %copy-done.60) | copy-start | bytes 3076
  227.0 94.3 %copy-start.63 = (f32[256,1]{0,1:T(1,128)S(1)}, f32[256,1]{0,1:T(1,128)}, u32[]{:S(2)}) copy-start(f32[256,1]{0,1:T(1,128)} %copy-done.62) | copy-start | bytes 3076
  227.0 94.3 %copy-start.65 = (f32[256,1]{0,1:T(1,128)S(1)}, f32[256,1]{0,1:T(1,128)}, u32[]{:S(2)}) copy-start(f32[256,1]{0,1:T(1,128)} %copy-done.64) | copy-start | bytes 3076
  227.0 94.3 %copy-start.67 = (f32[256,1]{0,1:T(1,128)S(1)}, f32[256,1]{0,1:T(1,128)}, u32[]{:S(2)}) copy-start(f32[256,1]{0,1:T(1,128)} %copy-done.66) | copy-start | bytes 3076
  227.0 161.3 %reduce-scatter.10.cloned.1.call-start = ((), (), s32[]{:S(2)}) async-start(), calls=%async_computation.10 | async-start | bytes 1179648 | tf_op jit(solution)/shard_map/reduce_scatter | solution.py:199
  323.6 122.1 %reduce-scatter.12.cloned.1.call-start = ((), (), s32[]{:S(2)}) async-start(), calls=%async_computation.11 | async-start | bytes 73728 | tf_op jit(solution)/shard_map/reduce_scatter | solution.py:200
  324.7 193.3 %reduce-scatter.14.cloned.1.call-start = ((), (), s32[]{:S(2)}) async-start(), calls=%async_computation.12 | async-start | bytes 2359296 | tf_op jit(solution)/shard_map/reduce_scatter | solution.py:201
  328.2 262.0 %reduce-scatter.8.cloned.1.call-start = ((), (), s32[]{:S(2)}) async-start(), calls=%async_computation.9 | async-start | bytes 2359296 | tf_op jit(solution)/shard_map/reduce_scatter | solution.py:193
  331.4 331.1 %reduce-scatter.6.cloned.1.call-start = ((), (), s32[]{:S(2)}) async-start(), calls=%async_computation.8 | async-start | bytes 2359296 | tf_op jit(solution)/shard_map/reduce_scatter | solution.py:187
  333.9 41.4 %copy-start.68 = (f32[512]{0:T(512)S(1)}, f32[512]{0:T(512)}, u32[]{:S(2)}) copy-start(f32[512]{0:T(512)} %get-tuple-element.140) | copy-start | bytes 6148
  (54 other events, 355.7 us)
Sparse Core Ops, SparseCore 0:
  10.1 43.5 all-gather.3
  55.8 39.1 all-gather.5
  97.1 38.3 all-gather.7
  227.1 92.4 all-reduce.27
  323.7 64.5 reduce-scatter.9
  391.8 53.8 reduce-scatter.11
  449.8 68.1 reduce-scatter.13
  522.1 68.0 reduce-scatter.7
  594.3 68.2 reduce-scatter.5
where the time goes:
time: 680 us; the launch traced here: 670 us
  waiting for transfers between devices  402 us (59%)
  blocking collectives  122 us (18%)
  matrix products  76.6 us (11%)
  other arithmetic  32.2 us (5%)
  local copies, waits for them, and re-layouts  21.5 us (3%)
  between operations  15.2 us (2%)
    psum x1, waiting for transfers between devices, on_device(): summed = lax.psum(partial_out, ('head', 'tensor'))  92.5 us
    reduce_scatter x1, waiting for transfers between devices, on_device(): lax.psum_scatter(g_w_x.reshape(model_width, head_count, head_width), 'fsd...  72.4 us
    reduce_scatter x1, waiting for transfers between devices, on_device(): lax.psum_scatter(g_w_out.reshape(head_count, head_width, model_width), 'f...  72.3 us
    reduce_scatter x1, waiting for transfers between devices, on_device(): lax.psum_scatter(g_w_z.reshape(model_width, head_count, head_width), 'fsd...  72.2 us
    reduce_scatter x1, waiting for transfers between devices, on_device(): lax.psum_scatter(g_w_dt, 'fsdp', scatter_dimension=0, tiled=True)  55.8 us
    psum x1, blocking collectives, on_device(): lax.psum((g_norm_gain, g_conv_x.reshape(head_count, head_width, taps), g_...  38.1 us
    all_gather x1, blocking collectives, on_device(): lax.all_gather(weights[2], 'fsdp', axis=0, tiled=True)  32 us
    all_gather x1, blocking collectives, on_device(): lax.all_gather(weights[3], 'fsdp', axis=0, tiled=True)  28.3 us
  transfers between devices with their start and end apart: 9, of which 7 were waited for; matrix products, arithmetic and copies ran while one was open for 7% of the time, Pallas kernels for 0%

commit v1 on v0

v1 whole, which is shorter than its diff:
```python
from functools import partial

import jax
import jax.numpy as jnp
from jax import lax
from jax.experimental import pallas as pl
from jax.experimental.pallas import tpu as pltpu
from jax.sharding import PartitionSpec as P

EPSILON = 1e-05
PRECISE = lax.Precision.HIGHEST
LANES = 128
CHUNK = 256
MESH = pl.DeviceIdType.MESH
VMEM_SPEC = pl.BlockSpec(memory_space=pltpu.VMEM)


def ring_index(position, count):
    high = position // (count // 2)
    return (1 - high) * 2 * position + high * (2 * (count - 1 - position) + 1)


def ring_position(index, count):
    odd = index % 2
    return (1 - odd) * (index // 2) + odd * (count - 1 - index // 2)


def ring_setup(count):
    me = lax.axis_index("fsdp")
    position = ring_position(me, count)
    right = ring_index((position + 1) % count, count)
    left = ring_index((position + count - 1) % count, count)
    barrier = pltpu.get_barrier_semaphore()
    for neighbour in (left, right):
        pl.semaphore_signal(barrier, inc=1, device_id={"fsdp": neighbour}, device_id_type=MESH)
    pl.semaphore_wait(barrier, 2)
    return me, position, (right, left)


def gather_kernel(count, split, x_ref, o_ref, local_sem, send_sem, recv_sem):
    me, position, targets = ring_setup(count)
    local = pltpu.make_async_copy(x_ref, o_ref.at[me], local_sem)
    local.start()
    width = x_ref.shape[1]
    columns = (pl.ds(0, split), pl.ds(split, width - split))
    copies = [[], []]
    for step in range(count - 1):
        for way in (0, 1):
            shift = count - step if way == 0 else step
            block = ring_index((position + shift) % count, count)
            target = o_ref.at[block, :, columns[way]]
            source = x_ref.at[:, columns[way]] if step == 0 else target
            if step > 0:
                copies[way][step - 1].wait_recv()
            copy = pltpu.make_async_remote_copy(
                src_ref=source,
                dst_ref=target,
                send_sem=send_sem.at[way, step],
                recv_sem=recv_sem.at[way, step],
                device_id={"fsdp": targets[way]},
                device_id_type=MESH,
            )
            copy.start()
            copies[way].append(copy)
    for way in (0, 1):
        copies[way][count - 2].wait_recv()
        for copy in copies[way]:
            copy.wait_send()
    local.wait()


def ring_gather(shard):
    count = lax.axis_size("fsdp")
    rows, width = shard.shape
    split = (width // LANES + 1) // 2 * LANES
    return pl.pallas_call(
        partial(gather_kernel, count, split),
        out_shape=jax.ShapeDtypeStruct((count, rows, width), shard.dtype),
        in_specs=[VMEM_SPEC],
        out_specs=pl.BlockSpec(memory_space=pl.ANY),
        scratch_shapes=[
            pltpu.SemaphoreType.DMA,
            pltpu.SemaphoreType.DMA((2, count - 1)),
            pltpu.SemaphoreType.DMA((2, count - 1)),
        ],
        compiler_params=pltpu.CompilerParams(collective_id=0, has_side_effects=True),
        name="ring_gather",
    )(shard).reshape(count * rows, width)


def scatter_kernel(count, split, g_ref, o_ref, up_ref, down_ref, send_sem, recv_sem):
    me, position, targets = ring_setup(count)
    width = g_ref.shape[2]
    columns = (pl.ds(0, split), pl.ds(split, width - split))
    slots = (up_ref, down_ref)
    copies = [[], []]
    for step in range(count - 1):
        for way in (0, 1):
            shift = 2 * count - 1 - step if way == 0 else 1 + step
            block = ring_index((position + shift) % count, count)
            if step == 0:
                source = g_ref.at[block, :, columns[way]]
            else:
                copies[way][step - 1].wait_recv()
                held = slots[way]
                held[step - 1] = (
                    held[step - 1].astype(jnp.float32)
                    + g_ref[block, :, columns[way]].astype(jnp.float32)
                ).astype(held.dtype)
                source = held.at[step - 1]
            copy = pltpu.make_async_remote_copy(
                src_ref=source,
                dst_ref=slots[way].at[step],
                send_sem=send_sem.at[way, step],
                recv_sem=recv_sem.at[way, step],
                device_id={"fsdp": targets[way]},
                device_id_type=MESH,
            )
            copy.start()
            copies[way].append(copy)
    for way in (0, 1):
        copies[way][count - 2].wait_recv()
        o_ref[:, columns[way]] = slots[way][count - 2].astype(jnp.float32) + g_ref[
            me, :, columns[way]
        ].astype(jnp.float32)
        for copy in copies[way]:
            copy.wait_send()


def ring_scatter(blocks):
    count, rows, width = blocks.shape
    split = (width // LANES + 1) // 2 * LANES
    return pl.pallas_call(
        partial(scatter_kernel, count, split),
        out_shape=jax.ShapeDtypeStruct((rows, width), jnp.float32),
        in_specs=[VMEM_SPEC],
        out_specs=VMEM_SPEC,
        scratch_shapes=[
            pltpu.VMEM((count - 1, rows, split), blocks.dtype),
            pltpu.VMEM((count - 1, rows, width - split), blocks.dtype),
            pltpu.SemaphoreType.DMA((2, count - 1)),
            pltpu.SemaphoreType.DMA((2, count - 1)),
        ],
        compiler_params=pltpu.CompilerParams(collective_id=1, has_side_effects=True),
        name="ring_scatter",
    )(blocks)


def group_peers(heads, tensors):
    head, tensor = lax.axis_index("head"), lax.axis_index("tensor")
    peers = []
    for offset in range(1, heads * tensors):
        peer_head = (head + offset // tensors) % heads
        peer_tensor = (tensor + offset % tensors) % tensors
        peers.append((peer_head, peer_tensor))
    return head * tensors + tensor, peers


def group_barrier(peers):
    barrier = pltpu.get_barrier_semaphore()
    for head, tensor in peers:
        pl.semaphore_signal(
            barrier, inc=1, device_id={"head": head, "tensor": tensor}, device_id_type=MESH
        )
    pl.semaphore_wait(barrier, len(peers))


def group_exchange(peers, source_of, target, send_sem, recv_sem):
    copies = []
    for place, (head, tensor) in enumerate(peers):
        copy = pltpu.make_async_remote_copy(
            src_ref=source_of(head, tensor),
            dst_ref=target,
            send_sem=send_sem.at[place],
            recv_sem=recv_sem.at[place],
            device_id={"head": head, "tensor": tensor},
            device_id_type=MESH,
        )
        copy.start()
        copies.append(copy)
    return copies


def group_sum_kernel(heads, tensors, scattered, x_ref, o_ref, held, send_sem, recv_sem):
    me, peers = group_peers(heads, tensors)
    group_barrier(peers)

    def source_of(head, tensor):
        return x_ref.at[head * tensors + tensor] if scattered else x_ref

    copies = group_exchange(peers, source_of, held.at[me], send_sem, recv_sem)
    held[me] = x_ref[me] if scattered else x_ref[...]
    for copy in copies:
        copy.wait_recv()
    total = held[0].astype(jnp.float32)
    for place in range(1, heads * tensors):
        total = total + held[place].astype(jnp.float32)
    o_ref[...] = total
    for copy in copies:
        copy.wait_send()


def group_sum(x, scattered, collective):
    heads, tensors = lax.axis_size("head"), lax.axis_size("tensor")
    size = heads * tensors
    shape = x.shape[1:] if scattered else x.shape
    return pl.pallas_call(
        partial(group_sum_kernel, heads, tensors, scattered),
        out_shape=jax.ShapeDtypeStruct(shape, jnp.float32),
        in_specs=[VMEM_SPEC],
        out_specs=VMEM_SPEC,
        scratch_shapes=[
            pltpu.VMEM((size,) + shape, x.dtype),
            pltpu.SemaphoreType.DMA((size - 1,)),
            pltpu.SemaphoreType.DMA((size - 1,)),
        ],
        compiler_params=pltpu.CompilerParams(collective_id=collective, has_side_effects=True),
        name=f"group_sum_{collective}",
    )(x)


def group_gather_kernel(heads, tensors, x_ref, o_ref, send_sem, recv_sem):
    me, peers = group_peers(heads, tensors)
    group_barrier(peers)
    copies = group_exchange(peers, lambda head, tensor: x_ref, o_ref.at[me], send_sem, recv_sem)
    o_ref[me] = x_ref[...]
    for copy in copies:
        copy.wait_recv()
    for copy in copies:
        copy.wait_send()


def group_gather(x, collective):
    heads, tensors = lax.axis_size("head"), lax.axis_size("tensor")
    size = heads * tensors
    return pl.pallas_call(
        partial(group_gather_kernel, heads, tensors),
        out_shape=jax.ShapeDtypeStruct((size,) + x.shape, x.dtype),
        in_specs=[VMEM_SPEC],
        out_specs=VMEM_SPEC,
        scratch_shapes=[
            pltpu.SemaphoreType.DMA((size - 1,)),
            pltpu.SemaphoreType.DMA((size - 1,)),
        ],
        compiler_params=pltpu.CompilerParams(collective_id=collective, has_side_effects=True),
        name=f"group_gather_{collective}",
    )(x)


def decay_tile(cums_col, cums_row, first_row, rows, columns):
    gap = cums_col - cums_row
    row = first_row + lax.broadcasted_iota(jnp.int32, (rows, columns), 0)
    column = lax.broadcasted_iota(jnp.int32, (rows, columns), 1)
    return jnp.exp(jnp.where(row >= column, gap, -1e30))


def last_axes(a, b):
    return lax.dot_general(a, b, (((1,), (1,)), ((), ())), preferred_element_type=jnp.float32)


def first_axes(a, b):
    return lax.dot_general(a, b, (((0,), (0,)), ((), ())), preferred_element_type=jnp.float32)


def mix_kernel(per, width, b_ref, c_ref, x_ref, step_ref, col_ref, row_ref, y_ref, scores):
    length = x_ref.shape[0]
    chunk = min(CHUNK, length)

    @pl.when(pl.program_id(0) == 0)
    def _():
        scores[...] = last_axes(c_ref[...], b_ref[...])

    for head in range(per):
        part = slice(head * width, (head + 1) * width)
        step = step_ref[0, :, head : head + 1]
        v = (x_ref[:, part].astype(jnp.float32) * step).astype(jnp.bfloat16)
        for first in range(0, length, chunk):
            seen = first + chunk
            decay = decay_tile(
                col_ref[0, first:seen, head : head + 1],
                row_ref[0, head : head + 1, :seen],
                first,
                chunk,
                seen,
            )
            a = (scores[first:seen, :seen] * decay).astype(jnp.bfloat16)
            y_ref[first:seen, part] = jnp.dot(a, v[:seen], preferred_element_type=jnp.float32)


def back_kernel(
    per, width, b_ref, c_ref, x_ref, dy_ref, y_ref, skip_ref, step_ref, col_ref, row_ref,
    dx_ref, dstep_ref, dcums_ref, db_ref, dc_ref, scores, d_scores, carried,
):
    length = x_ref.shape[0]
    chunk = min(CHUNK, length)

    @pl.when(pl.program_id(0) == 0)
    def _():
        scores[...] = last_axes(c_ref[...], b_ref[...])
        d_scores[...] = jnp.zeros_like(d_scores)

    for head in range(per):
        part = slice(head * width, (head + 1) * width)
        step = step_ref[0, :, head : head + 1]
        x = x_ref[:, part].astype(jnp.float32)
        v = (x * step).astype(jnp.bfloat16)
        dy = dy_ref[:, part]
        dy_low = dy.astype(jnp.bfloat16)
        carried[...] = jnp.zeros_like(carried)
        for first in range(0, length, chunk):
            seen = first + chunk
            decay = decay_tile(
                col_ref[0, first:seen, head : head + 1],
                row_ref[0, head : head + 1, :seen],
                first,
                chunk,
                seen,
            )
            a = (scores[first:seen, :seen] * decay).astype(jnp.bfloat16)
            carried[:seen] += first_axes(a, dy_low[first:seen])
            d_scores[first:seen, :seen] += last_axes(dy_low[first:seen], v[:seen]) * decay
        u = carried[...]
        dx_ref[:, part] = step * u + skip_ref[:, part] * dy
        dstep_ref[0, :, head : head + 1] = jnp.sum(x * u, axis=1, keepdims=True)
        dcums_ref[0, :, head : head + 1] = jnp.sum(
            dy_low.astype(jnp.float32) * y_ref[:, part] - v.astype(jnp.float32) * u,
            axis=1,
            keepdims=True,
        )

    @pl.when(pl.program_id(0) == pl.num_programs(0) - 1)
    def _():
        low = d_scores[...].astype(jnp.bfloat16)
        dc_ref[...] = jnp.dot(low, b_ref[...], preferred_element_type=jnp.float32)
        db_ref[...] = first_axes(low, c_ref[...])


def whole(shape):
    return pl.BlockSpec(shape, lambda i: (0,) * len(shape))


def head_specs(length, per, width, state):
    wide = pl.BlockSpec((length, per * width), lambda i: (0, i))
    col = pl.BlockSpec((1, length, per), lambda i: (i, 0, 0))
    row = pl.BlockSpec((1, per, length), lambda i: (i, 0, 0))
    return whole((length, state)), wide, col, row


def mix(b, c, x, step, col, row, width):
    length, inner = x.shape
    per = col.shape[2]
    maps, wide, col_spec, row_spec = head_specs(length, per, width, b.shape[1])
    return pl.pallas_call(
        partial(mix_kernel, per, width),
        grid=(inner // (per * width),),
        in_specs=[maps, maps, wide, col_spec, col_spec, row_spec],
        out_specs=wide,
        out_shape=jax.ShapeDtypeStruct((length, inner), jnp.float32),
        scratch_shapes=[pltpu.VMEM((length, length), jnp.float32)],
        name="mix",
    )(b, c, x, step, col, row)


def mix_back(b, c, x, dy, y, skip_row, step, col, row, width):
    length, inner = x.shape
    groups, _, per = col.shape
    state = b.shape[1]
    maps, wide, col_spec, row_spec = head_specs(length, per, width, state)
    return pl.pallas_call(
        partial(back_kernel, per, width),
        grid=(groups,),
        in_specs=[
            maps, maps, wide, wide, wide,
            pl.BlockSpec((1, per * width), lambda i: (0, i)),
            col_spec, col_spec, row_spec,
        ],
        out_specs=[wide, col_spec, col_spec, maps, maps],
        out_shape=[
            jax.ShapeDtypeStruct((length, inner), jnp.float32),
            jax.ShapeDtypeStruct((groups, length, per), jnp.float32),
            jax.ShapeDtypeStruct((groups, length, per), jnp.float32),
            jax.ShapeDtypeStruct((length, state), jnp.float32),
            jax.ShapeDtypeStruct((length, state), jnp.float32),
        ],
        scratch_shapes=[
            pltpu.VMEM((length, length), jnp.float32),
            pltpu.VMEM((length, length), jnp.float32),
            pltpu.VMEM((length, width), jnp.float32),
        ],
        name="mix_back",
    )(b, c, x, dy, y, skip_row, step, col, row)


def delayed(signal, count):
    return signal if count == 0 else jnp.pad(signal, ((count, 0), (0, 0)))[: signal.shape[0]]


def advanced(signal, count):
    return signal if count == 0 else jnp.pad(signal, ((0, count), (0, 0)))[count:]


def causal_conv(signal, kernel):
    taps = kernel.shape[1]
    return sum(delayed(signal, taps - 1 - k) * kernel[:, k] for k in range(taps))


def silu_slope(value):
    sigma = jax.nn.sigmoid(value)
    return sigma * (1.0 + value * (1.0 - sigma))


def conv_silu_back(raw, conv, kernel, upstream):
    taps = kernel.shape[1]
    d_conv = upstream * silu_slope(conv)
    d_raw = sum(advanced(d_conv, taps - 1 - k) * kernel[:, k] for k in range(taps))
    d_kernel = jnp.stack(
        [jnp.sum(delayed(raw, taps - 1 - k) * d_conv, axis=0) for k in range(taps)], axis=0
    )
    return d_raw, d_kernel


def pad_lanes(a):
    extra = -a.shape[-1] % LANES
    return a if extra == 0 else jnp.pad(a, ((0, 0),) * (a.ndim - 1) + ((0, extra),))


def on_device(
    block_in, cotangent, norm_gain, w_x, w_z, w_bc, w_dt, conv_x, conv_bc, dt_bias, a_log, skip,
    gate_gain, w_out,
):
    length, width = block_in.shape
    head_count, head_width, taps = conv_x.shape
    state = conv_bc.shape[1]
    inner = head_count * head_width
    heads, tensors, count = (lax.axis_size(a) for a in ("head", "tensor", "fsdp"))
    size = heads * tensors
    head_at = lax.axis_index("head")
    group_at = head_at * tensors + lax.axis_index("tensor")
    quarter = 2 * state // size
    rows = w_x.shape[0]
    owned = length // size
    full_inner = inner * size

    packed = jnp.concatenate(
        [
            w_x.reshape(rows, inner),
            w_z.reshape(rows, inner),
            w_bc.reshape(rows, 2 * state),
            pad_lanes(w_dt),
            w_out.reshape(inner, rows).T,
        ],
        axis=1,
    )
    weights = ring_gather(packed)
    dt_at = 2 * inner + 2 * state
    out_at = packed.shape[1] - inner
    weight_out = weights[:, out_at:]
    features = block_in.astype(jnp.float32)
    scale_in = lax.rsqrt(jnp.mean(features * features, axis=1, keepdims=True) + EPSILON)
    normed = (features * scale_in * norm_gain).astype(jnp.bfloat16)
    raw = jnp.dot(normed, weights[:, :out_at], preferred_element_type=jnp.float32)
    x_raw = raw[:, :inner]
    z_raw = raw[:, inner : 2 * inner]
    bc_raw = raw[:, 2 * inner : dt_at]
    dt_in = raw[:, dt_at : dt_at + head_count] + dt_bias
    kernel_x = conv_x.reshape(inner, taps)
    kernel_bc = conv_bc.reshape(2 * state, taps)
    gain = gate_gain.reshape(inner)
    x_conv = causal_conv(x_raw, kernel_x)
    x_act = jax.nn.silu(x_conv).astype(jnp.bfloat16)
    bc_act = jax.nn.silu(causal_conv(bc_raw, kernel_bc)).astype(jnp.bfloat16)
    b_maps, c_maps = bc_act[:, :state], bc_act[:, state:]

    per = max(1, LANES // head_width)
    step = jax.nn.softplus(dt_in)
    rate = -jnp.exp(a_log)
    at = jnp.arange(length)
    lower = (at[:, None] >= at[None, :]).astype(jnp.float32)
    cums = jnp.dot(lower, step * rate, precision=PRECISE)

    def as_columns(a):
        return a.reshape(length, head_count // per, per).transpose(1, 0, 2)

    def from_columns(a):
        return a.transpose(1, 0, 2).reshape(length, head_count)

    step_col = as_columns(step)
    col = as_columns(cums)
    row = cums.T.reshape(head_count // per, per, length)
    scanned = mix(b_maps, c_maps, x_act, step_col, col, row, head_width)
    skip_row = jnp.repeat(skip, head_width)[None, :]
    x_wide = x_act.astype(jnp.float32)
    mixed = scanned + skip_row * x_wide
    z_sigma = jax.nn.sigmoid(z_raw)
    z_silu = z_raw * z_sigma
    gated = mixed * z_silu
    d_normed_out = jnp.dot(cotangent, weight_out, preferred_element_type=jnp.float32)
    d_hat = d_normed_out * gain
    sums = jnp.concatenate([jnp.sum(gated * gated, axis=1), jnp.sum(d_hat * gated, axis=1)])
    sums = group_sum(sums.reshape(-1, LANES), False, 2).reshape(2, length)
    scale_out = lax.rsqrt(sums[0] / full_inner + EPSILON)[:, None]
    inner_sum = sums[1][:, None]
    normed_out = (gated * scale_out * gain).astype(jnp.bfloat16)
    partial_out = last_axes(normed_out, weight_out).astype(jnp.bfloat16)
    mine = lambda a: lax.dynamic_slice_in_dim(a, group_at * owned, owned, 0)
    summed = group_sum(partial_out.reshape(size, owned, width), True, 3)
    own_out = (summed + mine(features)).astype(jnp.bfloat16)
    block_out = group_gather(own_out, 4).reshape(length, width)

    g_gate_gain = jnp.sum(d_normed_out * gated * scale_out, axis=0)
    d_gated = scale_out * d_hat - gated * scale_out**3 * (inner_sum / full_inner)
    d_mixed = d_gated * z_silu
    d_z = (d_gated * mixed * (z_sigma * (1.0 + z_raw * (1.0 - z_sigma)))).astype(jnp.bfloat16)
    d_xs, d_step, d_cums, d_b, d_c = mix_back(
        b_maps, c_maps, x_act, d_mixed, scanned, skip_row, step_col, col, row, head_width
    )
    d_logs = jnp.dot(lower.T, from_columns(d_cums), precision=PRECISE)
    d_step = from_columns(d_step) + d_logs * rate
    d_dt_part = d_step * jax.nn.sigmoid(dt_in)
    g_a_log = jnp.sum(d_logs * step, axis=0) * rate
    g_skip = jnp.sum((d_mixed * x_wide).reshape(length, head_count, head_width), axis=(0, 2))

    d_bc_part = jnp.concatenate([d_b, d_c], axis=1)
    pieces = []
    for place in range(size):
        same = (head_at == place // tensors).astype(jnp.float32)
        pieces.append(
            pad_lanes(
                jnp.concatenate(
                    [d_bc_part[:, place * quarter : (place + 1) * quarter], d_dt_part * same], axis=1
                )
            )
        )
    d_small = group_sum(jnp.stack(pieces).astype(jnp.bfloat16), True, 5)
    d_bc = d_small[:, :quarter]
    d_dt = d_small[:, quarter : quarter + head_count]
    g_dt_bias = jnp.sum(d_dt, axis=0)

    own_cols = lambda a, axis: lax.dynamic_slice_in_dim(a, group_at * quarter, quarter, axis)
    bc_raw_own = own_cols(bc_raw, 1)
    kernel_bc_own = own_cols(kernel_bc, 0)
    d_bc_raw, g_conv_bc = conv_silu_back(
        bc_raw_own, causal_conv(bc_raw_own, kernel_bc_own), kernel_bc_own, d_bc
    )
    d_x_raw, g_conv_x = conv_silu_back(x_raw, x_conv, kernel_x, d_xs)
    d_cat = jnp.concatenate(
        [
            d_x_raw.astype(jnp.bfloat16),
            d_z,
            pad_lanes(jnp.concatenate([d_bc_raw, d_dt], axis=1).astype(jnp.bfloat16)),
        ],
        axis=1,
    )
    only = (lax.axis_index("tensor") == 0).astype(jnp.bfloat16)
    side = pad_lanes(
        jnp.concatenate(
            [own_cols(weights[:, 2 * inner : dt_at], 1), weights[:, dt_at : dt_at + head_count] * only],
            axis=1,
        )
    )
    local_part = last_axes(d_cat[:, : 2 * inner], weights[:, : 2 * inner]) + last_axes(
        d_cat[:, 2 * inner :], side
    )
    d_normed = group_sum(local_part.astype(jnp.bfloat16).reshape(size, owned, width), True, 6)
    own_features, own_scale = mine(features), mine(scale_in)
    g_norm_gain = jnp.sum(d_normed * own_features * own_scale, axis=0)
    d_in_hat = d_normed * norm_gain
    own_grad = own_scale * d_in_hat - own_features * own_scale**3 * jnp.mean(
        d_in_hat * own_features, axis=1, keepdims=True
    )
    others = group_gather(own_grad.astype(jnp.bfloat16), 7).reshape(length, width)
    grad_in = others.astype(jnp.float32) + cotangent.astype(jnp.float32)

    grads = jnp.concatenate(
        [
            first_axes(normed, d_cat).astype(jnp.bfloat16),
            first_axes(cotangent, normed_out).astype(jnp.bfloat16),
        ],
        axis=1,
    )
    own = ring_scatter(grads.reshape(count, rows, grads.shape[1]))
    side_at = 2 * inner
    g_w_bc = group_gather(pad_lanes(own[:, side_at : side_at + quarter]), 8)[:, :, :quarter]
    g_w_bc = g_w_bc.transpose(1, 0, 2).reshape(rows, 2, state)

    small = lax.psum(
        jnp.concatenate(
            [g_norm_gain, g_conv_x.reshape(-1), g_gate_gain, g_conv_bc.reshape(-1), g_dt_bias, g_a_log, g_skip]
        ),
        "fsdp",
    )
    cuts = []
    start = 0
    for amount in (width, taps * inner, inner, taps * quarter, head_count, head_count, head_count):
        cuts.append(small[start : start + amount])
        start += amount
    spread = jnp.zeros((2 * state, taps), jnp.float32)
    spread = lax.dynamic_update_slice_in_dim(
        spread, cuts[3].reshape(taps, quarter).T, group_at * quarter, 0
    )
    by_head = jnp.zeros((heads, 2 * head_count), jnp.float32)
    by_head = lax.dynamic_update_slice_in_dim(
        by_head, jnp.concatenate([cuts[5], cuts[6]])[None], head_at, 0
    )
    last = jnp.concatenate([cuts[0], spread.reshape(-1), by_head.reshape(-1)])
    total = last.shape[0]
    last = jnp.pad(last, (0, -total % (8 * LANES))).reshape(-1, LANES)
    last = group_sum(last, False, 9).reshape(-1)
    at_heads = width + 2 * state * taps
    mine_head = lax.dynamic_slice_in_dim(
        last[at_heads:total].reshape(heads, 2 * head_count), head_at, 1, 0
    )[0]
    return (
        block_out,
        grad_in,
        last[:width],
        own[:, :inner].reshape(rows, head_count, head_width),
        own[:, inner : 2 * inner].reshape(rows, head_count, head_width),
        g_w_bc,
        own[:, side_at + quarter : side_at + quarter + head_count],
        cuts[1].reshape(taps, inner).T.reshape(head_count, head_width, taps),
        last[width:at_heads].reshape(2, state, taps),
        cuts[4],
        mine_head[:head_count],
        mine_head[head_count:],
        cuts[2].reshape(head_count, head_width),
        own[:, own.shape[1] - inner :].T.reshape(head_count, head_width, rows),
    )


def solution(mesh):
    return jax.shard_map(
        on_device,
        mesh=mesh,
        in_specs=(
            P("fsdp", None),
            P("fsdp", None),
            P(),
            P("fsdp", "head", "tensor"),
            P("fsdp", "head", "tensor"),
            P("fsdp", None, None),
            P("fsdp", "head"),
            P("head", "tensor", None),
            P(),
            P("head"),
            P("head"),
            P("head"),
            P("head", "tensor"),
            P("head", "tensor", "fsdp"),
        ),
        out_specs=(
            P("fsdp", None),
            P("fsdp", None),
            P(),
            P("fsdp", "head", "tensor"),
            P("fsdp", "head", "tensor"),
            P("fsdp", None, None),
            P("fsdp", "head"),
            P("head", "tensor", None),
            P(),
            P("head"),
            P("head"),
            P("head"),
            P("head", "tensor"),
            P("head", "tensor", "fsdp"),
        ),
        check_vma=False,
    )
```

time: 680 us -> 344 us (0.51); the launches traced: 670 us -> 343 us
  waiting for transfers between devices: 402 us -> 0 us
  Pallas kernels: 0 us -> 224 us
  blocking collectives: 122 us -> 35.7 us
  matrix products: 76.6 us -> 20.5 us
  local copies, waits for them, and re-layouts: 21.5 us -> 35.4 us
  between operations: 15.2 us -> 1.35 us
    reduce_scatter x5 -> x0, waiting for transfers between devices: 281 us -> none  [the longest x1 72.4 us: on_device(): lax.psum_scatter(g_w_x.reshape(model_width, head_count, head_width), 'fsd...]
    pallas_call x0 -> x12, Pallas kernels: none -> 224 us  [the longest x1 54.7 us: ring_gather(): pl.pallas_call(partial(gather_kernel, count, split), out_shape=jax.ShapeD...]
    psum x1 -> x0, waiting for transfers between devices: 92.5 us -> none  [on_device(): summed = lax.psum(partial_out, ('head', 'tensor'))]
    all_gather x2 -> x0, blocking collectives: 60.3 us -> none  [the longest x1 32 us: on_device(): lax.all_gather(weights[2], 'fsdp', axis=0, tiled=True)]
    dot_general x25 -> x9, matrix products: 74.3 us -> 20.5 us  [the longest x3 7.64 us: last_axes(): lax.dot_general(a, b, (((1,), (1,)), ((), ())), preferred_element_type=jn...]
    all_gather x3 -> x0, waiting for transfers between devices: 26 us -> none  [the longest x1 26 us: on_device(): lax.all_gather(weights[4], 'fsdp', axis=2, tiled=True)]
    psum x4 -> x1, blocking collectives: 61.4 us -> 35.7 us  [on_device(): lax.psum(jnp.concatenate([g_norm_gain, g_conv_x.reshape(-1), g_gate_gain,...]
    slice x5 -> x23, local copies, waits for them, and re-layouts: 0.35 us -> 9.22 us  [the longest x1 1.27 us: on_device(): last[width:at_heads].reshape(2, state, taps)]
  transfers between devices with their start and end apart: 9 -> 0, of which waited for: 7 -> 0; matrix products, arithmetic and copies ran while one was open for 7% -> 0% of each run, Pallas kernels for 0% -> 0%
where the time goes in v1:
time: 344 us; the launch traced here: 343 us
  Pallas kernels  224 us (65%)
  blocking collectives  35.7 us (10%)
  local copies, waits for them, and re-layouts  35.4 us (10%)
  other arithmetic  26 us (8%)
  matrix products  20.5 us (6%)
    pallas_call x1, Pallas kernels, ring_gather(): pl.pallas_call(partial(gather_kernel, count, split), out_shape=jax.ShapeD...  54.7 us
    pallas_call x5, Pallas kernels, group_sum(): pl.pallas_call(partial(group_sum_kernel, heads, tensors, scattered), out_...  51.6 us
    pallas_call x1, Pallas kernels, ring_scatter(): pl.pallas_call(partial(scatter_kernel, count, split), out_shape=jax.Shape...  47.8 us
    pallas_call x3, Pallas kernels, group_gather(): pl.pallas_call(partial(group_gather_kernel, heads, tensors), out_shape=ja...  38.1 us
    psum x1, blocking collectives, on_device(): lax.psum(jnp.concatenate([g_norm_gain, g_conv_x.reshape(-1), g_gate_gain,...  35.7 us
    pallas_call x1, Pallas kernels, mix_back(): pl.pallas_call(partial(back_kernel, per, width), grid=(groups,), in_specs...  21 us
    pallas_call x1, Pallas kernels, mix(): pl.pallas_call(partial(mix_kernel, per, width), grid=(inner // (per * wid...  10.9 us
    unnamed x60, local copies, waits for them, and re-layouts  9.8 us

profile of v1, /device:TPU:0, one launch (start us, length us, event | category | flops | bytes accessed | tf_op | source)
XLA Modules:
  0.0 343.0 jit_solution(3278054087896081578)
XLA Ops:
  6.2 54.7 %ring_gather.1 = bf16[8,128,1920]{2,1,0:T(8,128)(2,1)} custom-call(bf16[128,1920]{1,0:T(8,128)(2,1)} %copy-done.13), custom_call_target="tpu_custom_call" | custom-call | tf_op jit(solution)/shard_map/ring_gather/pallas_call | solution.py:76
  61.2 3.7 %fusion = f32[512,1408]{1,0:T(8,128)S(1)} fusion(bf16[1024,1920]{1,0:T(8,128)(2,1)} %bitcast.114, f32[1024]{0:T(1024)S(1)} %copy-done.18, f32[512]{0:T(512)S(1)} %add_rsqrt_fusion, bf16[512,1024]{1,0:T(8,128)(2,1)S(1)} %copy-done.4), kind=kOutput, calls=%fused_computation.2 | convolution fusion | flops 1478492160 | bytes 6821888 | tf_op jit(solution)/shard_map/dot_general | solution.py:461
  64.9 1.6 copy-done.2
  67.4 1.8 multiply_convert_fusion.3
  73.0 1.4 copy.99
  76.6 10.9 %mix.1.y_ref = f32[512,512]{1,0:T(8,128)} custom-call(bf16[512,128]{1,0:T(8,128)(2,1)} %get-tuple-element.112.b_ref, bf16[512,128]{1,0:T(8,128)(2,1)} %get-tuple-element.111.c_ref, bf16[512,512]{1,0:T(8,128)(2,1)} %get-tuple-element.101.x_ref, f32[4,512,4]{2,1,0:T(8,128)} %bitcast.112, f32[4,512,4]{2,1,0:T(8,128)} %bitcast.110, f32[4,4,512]{2,1,0:T(4,128)} %reshape.221.row_ref), custom_call_target="tpu_custom_call" | custom-call | tf_op jit(solution)/shard_map/mix/pallas_call | solution.py:353
  87.7 4.5 %multiply_reduce_fusion.7 = (f32[512]{0:T(512)S(1)}, f32[512]{0:T(512)S(1)}, f32[512,512]{1,0:T(8,128)}, f32[512,512]{1,0:T(8,128)}) fusion(f32[512]{0:T(512)S(1)} %mul.476, f32[512,1408]{1,0:T(8,128)} %copy-done.2, f32[512,512]{1,0:T(8,128)} %mix.1.y_ref, bf16[512,512]{1,0:T(8,128)(2,1)S(1)} %copy-done.1, f32[512]{0:T(512)S(1)} %mul.470, ...), kind=kOutput, calls=%fused_computation.49 | convolution fusion | flops 540277760 | bytes 6823936 | tf_op jit(solution)/shard_map/dot_general | solution.py:497
  92.8 4.9 %group_sum_2.1 = f32[8,128]{1,0:T(8,128)} custom-call(f32[8,128]{1,0:T(8,128)} %pad_maximum_fusion.6.x_ref), custom_call_target="tpu_custom_call" | custom-call | tf_op jit(solution)/shard_map/group_sum_2/pallas_call | solution.py:207
  99.2 4.0 %fusion.18 = (f32[512]{0:T(512)S(1)}, f32[512,512]{1,0:T(8,128)}, bf16[512,512]{1,0:T(8,128)(2,1)}, f32[512]{0:T(512)S(1)}) fusion(bf16[512,512]{1,0:T(8,128)(2,1)S(1)} %copy-done.1, f32[512,1408]{1,0:T(8,128)} %copy-done.2, f32[512]{0:T(512)S(1)} %get-tuple-element.127, f32[512,512]{1,0:T(8,128)} %get-tuple-element.100, f32[512]{0:T(512)S(1)} %multiply_multiply_fusion.2, ...), kind=kLoop, calls=%fused_computation.35 | loop fusion | flops 6552576 | bytes 6305792 | tf_op jit(solution)/shard_map/reduce_sum | solution.py:521
  103.9 21.0 %mix_back.1 = (f32[512,512]{1,0:T(8,128)}, f32[4,512,4]{2,1,0:T(8,128)}, f32[4,512,4]{2,1,0:T(8,128)}, f32[512,128]{1,0:T(8,128)}, f32[512,128]{1,0:T(8,128)}) custom-call(bf16[512,128]{1,0:T(8,128)(2,1)} %get-tuple-element.112.b_ref, bf16[512,128]{1,0:T(8,128)(2,1)} %get-tuple-element.111.c_ref, bf16[512,512]{1,0:T(8,128)(2,1)} %get-tuple-element.101.x_ref, ...), custom_call_target="tpu_custom_call" | custom-call | tf_op jit(solution)/shard_map/mix_back/pallas_call | solution.py:369
  124.9 1.7 copy.101
  127.8 1.7 multiply_convert_fusion.8
  131.1 9.9 %group_sum_5.1 = f32[512,128]{1,0:T(8,128)} custom-call(bf16[4,512,128]{2,1,0:T(8,128)(2,1)} %pad_maximum_fusion.1.x_ref), custom_call_target="tpu_custom_call" | custom-call | tf_op jit(solution)/shard_map/group_sum_5/pallas_call | solution.py:207
  141.3 1.4 multiply_reduce_fusion.14
  144.0 2.1 multiply_reduce_fusion.5
  146.7 1.7 convolution_convert_fusion
  149.2 2.0 pad_maximum_fusion
  151.2 47.8 %ring_scatter.1 = f32[128,1664]{1,0:T(8,128)} custom-call(bf16[8,128,1664]{2,1,0:T(8,128)(2,1)} %bitcast.109), custom_call_target="tpu_custom_call" | custom-call | tf_op jit(solution)/shard_map/ring_scatter/pallas_call | solution.py:133
  203.4 6.8 %group_gather_8.1 = f32[4,128,128]{2,1,0:T(8,128)} custom-call(f32[128,128]{1,0:T(8,128)} %pad.126.x_ref), custom_call_target="tpu_custom_call" | custom-call | tf_op jit(solution)/shard_map/group_gather_8/pallas_call | solution.py:236
  212.9 2.9 fusion.2
  218.0 1.5 add_convert_fusion
  219.5 15.8 %group_sum_6.1 = f32[128,1024]{1,0:T(8,128)} custom-call(bf16[4,128,1024]{2,1,0:T(8,128)(2,1)} %bitcast.121), custom_call_target="tpu_custom_call" | custom-call | tf_op jit(solution)/shard_map/group_sum_6/pallas_call | solution.py:207
  235.5 1.5 convert_element_type.119
  237.6 35.7 %psum.7 = f32[3888]{0:T(1024)S(1)} all-reduce(f32[3888]{0:T(1024)S(1)} %concatenate.63), channel_id=1, replica_groups=mesh['fsdp'=8,'head'=2,'tensor'=2] {'fsdp'}, use_global_device_ids=true, to_apply=%region_18.19 | all-reduce | flops 3888 | bytes 31104 | tf_op jit(solution)/shard_map/psum | solution.py:586
  274.5 5.1 %group_sum_9.1 = f32[24,128]{1,0:T(8,128)} custom-call(f32[24,128]{1,0:T(8,128)} %fusion.58.x_ref), custom_call_target="tpu_custom_call" | custom-call | tf_op jit(solution)/shard_map/group_sum_9/pallas_call | solution.py:207
  285.0 3.3 convolution_convert_fusion.2
  288.3 15.8 %group_sum_3.1 = f32[128,1024]{1,0:T(8,128)} custom-call(bf16[4,128,1024]{2,1,0:T(8,128)(2,1)} %bitcast.122), custom_call_target="tpu_custom_call" | custom-call | tf_op jit(solution)/shard_map/group_sum_3/pallas_call | solution.py:207
  304.1 2.0 subtract_convert_fusion
  306.2 15.6 %group_gather_7.1 = bf16[4,128,1024]{2,1,0:T(8,128)(2,1)} custom-call(bf16[128,1024]{1,0:T(8,128)(2,1)} %get-tuple-element.105.x_ref), custom_call_target="tpu_custom_call" | custom-call | tf_op jit(solution)/shard_map/group_gather_7/pallas_call | solution.py:236
  321.8 3.2 convert_add_fusion
  325.1 15.6 %group_gather_4.1 = bf16[4,128,1024]{2,1,0:T(8,128)(2,1)} custom-call(bf16[128,1024]{1,0:T(8,128)(2,1)} %get-tuple-element.106.x_ref), custom_call_target="tpu_custom_call" | custom-call | tf_op jit(solution)/shard_map/group_gather_4/pallas_call | solution.py:236
  340.7 2.3 copy.129
  (156 shorter events, 37.5 us)
Async XLA Ops:
  5.4 0.8 copy-start.13
  6.2 54.7 %copy-start.4 = (bf16[512,1024]{1,0:T(8,128)(2,1)S(1)}, bf16[512,1024]{1,0:T(8,128)(2,1)}, u32[]{:S(2)}) copy-start(bf16[512,1024]{1,0:T(8,128)(2,1)} %param.14) | copy-start | bytes 3145732
  6.2 55.0 %copy-start.18 = (f32[1024]{0:T(1024)S(1)}, f32[1024]{0:T(1024)}, u32[]{:S(2)}) copy-start(f32[1024]{0:T(1024)} %param.16) | copy-start | bytes 12292
  64.9 1.6 copy-start.2
  66.5 0.8 copy-start.17
  67.3 3.0 copy-start.19
  67.4 4.0 %copy-start.21 = (f32[16]{0:T(128)S(1)}, f32[16]{0:T(128)}, u32[]{:S(2)}) copy-start(f32[16]{0:T(128)} %param.23) | copy-start | bytes 196
  69.2 3.3 copy-start.23
  76.6 10.9 %copy-start.20 = (f32[16,32]{1,0:T(8,128)S(1)}, f32[16,32]{1,0:T(8,128)}, u32[]{:S(2)}) copy-start(f32[16,32]{1,0:T(8,128)} %param.26) | copy-start | bytes 6148
  76.6 10.9 %copy-start.22 = (f32[16]{0:T(128)S(1)}, f32[16]{0:T(128)}, u32[]{:S(2)}) copy-start(f32[16]{0:T(128)} %param.25) | copy-start | bytes 196
  76.6 11.1 %copy-start.1 = (bf16[512,512]{1,0:T(8,128)(2,1)S(1)}, bf16[512,512]{1,0:T(8,128)(2,1)}, u32[]{:S(2)}) copy-start(bf16[512,512]{1,0:T(8,128)(2,1)} %get-tuple-element.101.x_ref) | copy-start | bytes 1572868
  87.7 11.5 %copy-start = (f32[512,512]{1,0:T(8,128)S(1)}, f32[512,512]{1,0:T(8,128)}, u32[]{:S(2)}) copy-start(f32[512,512]{1,0:T(8,128)} %mix.1.y_ref) | copy-start | bytes 3145732
  124.9 2.5 copy-start.12
  124.9 4.6 %copy-start.16 = (f32[512,128]{1,0:T(8,128)S(1)}, f32[512,128]{1,0:T(8,128)}, u32[]{:S(2)}) copy-start(f32[512,128]{1,0:T(8,128)} %get-tuple-element.20) | copy-start | bytes 786436
  127.8 2.1 copy-start.15
  130.2 13.7 %copy-start.7 = (f32[512,512]{1,0:T(8,128)S(1)}, f32[512,512]{1,0:T(8,128)}, u32[]{:S(2)}) copy-start(f32[512,512]{1,0:T(8,128)} %get-tuple-element.102) | copy-start | bytes 3145732
  141.0 2.9 copy-start.11
  144.0 2.6 copy-start.5
  144.0 2.6 copy-start.14
  146.6 1.7 copy-start.6
  146.6 1.7 copy-start.8
  199.0 3.8 %slice-start = ((f32[128,1664]{1,0:T(8,128)}), f32[128,64]{1,0:T(8,128)S(1)}, s32[]{:S(2)}) async-start(f32[128,1664]{1,0:T(8,128)} %ring_scatter.1), calls=%async_computation | async-start | bytes 131072 | tf_op jit(solution)/shard_map/slice | solution.py:583
  199.0 13.1 %copy-start.9 = (f32[128,1664]{1,0:T(8,128)S(1)}, f32[128,1664]{1,0:T(8,128)}, u32[]{:S(2)}) copy-start(f32[128,1664]{1,0:T(8,128)} %ring_scatter.1) | copy-start | bytes 2555908
  235.4 1.6 copy-start.3
  235.5 1.7 copy-start.10

commit v2 on v1

--- a/solution.py
+++ b/solution.py
@@ -11,6 +11,7 @@
 PRECISE = lax.Precision.HIGHEST
 LANES = 128
 CHUNK = 256
+WAYS = 4
 MESH = pl.DeviceIdType.MESH
 VMEM_SPEC = pl.BlockSpec(memory_space=pltpu.VMEM)
 
@@ -37,19 +38,30 @@
     return me, position, (right, left)
 
 
-def gather_kernel(count, split, x_ref, o_ref, local_sem, send_sem, recv_sem):
+def column_ways(width):
+    tiles = width // LANES
+    share, extra = tiles // WAYS, tiles % WAYS
+    cuts, start = [], 0
+    for way in range(WAYS):
+        amount = (share + (1 if way < extra else 0)) * LANES
+        cuts.append((start, amount))
+        start += amount
+    return cuts
+
+
+def gather_kernel(count, x_ref, o_ref, local_sem, send_sem, recv_sem):
     me, position, targets = ring_setup(count)
     local = pltpu.make_async_copy(x_ref, o_ref.at[me], local_sem)
     local.start()
-    width = x_ref.shape[1]
-    columns = (pl.ds(0, split), pl.ds(split, width - split))
-    copies = [[], []]
+    ways = column_ways(x_ref.shape[1])
+    copies = [[] for _ in ways]
     for step in range(count - 1):
-        for way in (0, 1):
-            shift = count - step if way == 0 else step
+        for way, (start, amount) in enumerate(ways):
+            shift = count - step if way % 2 == 0 else step
             block = ring_index((position + shift) % count, count)
-            target = o_ref.at[block, :, columns[way]]
-            source = x_ref.at[:, columns[way]] if step == 0 else target
+            columns = pl.ds(start, amount)
+            target = o_ref.at[block, :, columns]
+            source = x_ref.at[:, columns] if step == 0 else target
             if step > 0:
                 copies[way][step - 1].wait_recv()
             copy = pltpu.make_async_remote_copy(
@@ -57,12 +69,12 @@
                 dst_ref=target,
                 send_sem=send_sem.at[way, step],
                 recv_sem=recv_sem.at[way, step],
-                device_id={"fsdp": targets[way]},
+                device_id={"fsdp": targets[way % 2]},
                 device_id_type=MESH,
             )
             copy.start()
             copies[way].append(copy)
-    for way in (0, 1):
+    for way in range(len(ways)):
         copies[way][count - 2].wait_recv()
         for copy in copies[way]:
             copy.wait_send()
@@ -72,78 +84,276 @@
 def ring_gather(shard):
     count = lax.axis_size("fsdp")
     rows, width = shard.shape
-    split = (width // LANES + 1) // 2 * LANES
     return pl.pallas_call(
-        partial(gather_kernel, count, split),
+        partial(gather_kernel, count),
         out_shape=jax.ShapeDtypeStruct((count, rows, width), shard.dtype),
         in_specs=[VMEM_SPEC],
         out_specs=pl.BlockSpec(memory_space=pl.ANY),
         scratch_shapes=[
             pltpu.SemaphoreType.DMA,
-            pltpu.SemaphoreType.DMA((2, count - 1)),
-            pltpu.SemaphoreType.DMA((2, count - 1)),
+            pltpu.SemaphoreType.DMA((WAYS, count - 1)),
+            pltpu.SemaphoreType.DMA((WAYS, count - 1)),
         ],
         compiler_params=pltpu.CompilerParams(collective_id=0, has_side_effects=True),
         name="ring_gather",
     )(shard).reshape(count * rows, width)
 
 
-def scatter_kernel(count, split, g_ref, o_ref, up_ref, down_ref, send_sem, recv_sem):
-    me, position, targets = ring_setup(count)
-    width = g_ref.shape[2]
-    columns = (pl.ds(0, split), pl.ds(split, width - split))
-    slots = (up_ref, down_ref)
-    copies = [[], []]
+def send(source, target, sems, place, device):
+    copy = pltpu.make_async_remote_copy(
+        src_ref=source,
+        dst_ref=target,
+        send_sem=sems[0].at[place],
+        recv_sem=sems[1].at[place],
+        device_id=device,
+        device_id_type=MESH,
+    )
+    copy.start()
+    return copy
+
+
+def closing_kernel(
+    count, heads, tensors, side_at,
+    g_ref, dn_ref, po_ref, feat_ref, scale_ref, gain_ref, lone_ref, shared_ref,
+    own_ref, out_ref, grad_ref, bc_ref, lone_out, shared_out, norm_out,
+    *scratch,
+):
+    slots = scratch[:WAYS]
+    (held_a, stage, held_b, norm_own, norm_held, norm_sum, shared_held, shared_sum,
+     lone_all, shared_all, norm_all) = scratch[WAYS : WAYS + 11]
+    sem = scratch[WAYS + 11 :]
+    pairs = [(sem[2 * i], sem[2 * i + 1]) for i in range(len(sem) // 2)]
+    ring_sems, a_sems, b_sems, at_sems, ah_sems, group_sems, lone_sems, late_sems, bc_sems = pairs
+    me = lax.axis_index("fsdp")
+    position = ring_position(me, count)
+    targets = (
+        ring_index((position + 1) % count, count),
+        ring_index((position + count - 1) % count, count),
+    )
+    group_me, peers = group_peers(heads, tensors)
+    head, tensor = lax.axis_index("head"), lax.axis_index("tensor")
+    others = [(me + offset) % count for offset in range(1, count)]
+    barrier = pltpu.get_barrier_semaphore()
+    for h, t in peers:
+        pl.semaphore_signal(barrier, inc=1, device_id={"head": h, "tensor": t}, device_id_type=MESH)
+    for other in others:
+        pl.semaphore_signal(barrier, inc=1, device_id={"fsdp": other}, device_id_type=MESH)
+    pl.semaphore_wait(barrier, len(peers) + len(others))
+
+    started = []
+
+    def sent(*args):
+        copy = send(*args)
+        started.append(copy)
+        return copy
+
+    head_peers = [(head + offset) % heads for offset in range(1, heads)]
+    tensor_peers = [(tensor + offset) % tensors for offset in range(1, tensors)]
+    parts = (dn_ref, po_ref)
+    results = (grad_ref, out_ref)
+    phase = {}
+
+    def start_a():
+        for i, ref in enumerate(parts):
+            phase["a", i] = [
+                sent(
+                    ref.at[pl.ds(peer * tensors, tensors)], held_a.at[i, k], a_sems, (i, k),
+                    {"head": peer},
+                )
+                for k, peer in enumerate(head_peers)
+            ]
+        phase["lone"] = [
+            sent(lone_ref, lone_all.at[me], lone_sems, k, {"fsdp": other})
+            for k, other in enumerate(others)
+        ]
+        lone_all[me] = lone_ref[...]
+
+    def to_b(i):
+        for copy in phase["a", i]:
+            copy.wait_recv()
+        for t in range(tensors):
+            total = parts[i][head * tensors + t].astype(jnp.float32)
+            for k in range(heads - 1):
+                total = total + held_a[i, k, t].astype(jnp.float32)
+            stage[i, t] = total.astype(stage.dtype)
+        phase["b", i] = [
+            sent(stage.at[i, peer], held_b.at[i, k], b_sems, (i, k), {"tensor": peer})
+            for k, peer in enumerate(tensor_peers)
+        ]
+
+    def spread(i):
+        for copy in phase["b", i]:
+            copy.wait_recv()
+        total = stage[i, tensor].astype(jnp.float32)
+        for k in range(tensors - 1):
+            total = total + held_b[i, k].astype(jnp.float32)
+        features = feat_ref[...]
+        if i == 0:
+            scale = scale_ref[...]
+            norm_own[...] = jnp.sum(total * (features * scale), axis=0, keepdims=True)
+            inner = total * gain_ref[...]
+            mean = jnp.mean(inner * features, axis=1, keepdims=True)
+            value = scale * inner - features * (scale * scale * scale * mean)
+        else:
+            value = total + features
+        result = results[i]
+        result[group_me] = value.astype(result.dtype)
+        mine = result.at[group_me]
+        phase["t", i] = [
+            sent(mine, mine, at_sems, (i, k), {"tensor": peer}) for k, peer in enumerate(tensor_peers)
+        ]
+        phase["h", i] = [
+            sent(mine, mine, ah_sems, (i, k, 0), {"head": peer}) for k, peer in enumerate(head_peers)
+        ]
+        if i == 0:
+            norm_held[group_me] = norm_own[...]
+            shared_held[group_me] = shared_ref[...]
+            phase["group"] = []
+            for k, (h, t) in enumerate(peers):
+                device = {"head": h, "tensor": t}
+                phase["group"] += [
+                    sent(norm_own, norm_held.at[group_me], group_sems, (0, k), device),
+                    sent(shared_ref, shared_held.at[group_me], group_sems, (1, k), device),
+                ]
+
+    def forward(i):
+        result = results[i]
+        for k, copy in enumerate(phase["t", i]):
+            copy.wait_recv()
+            block = result.at[head * tensors + (tensor + tensors - 1 - k) % tensors]
+            phase["h", i] += [
+                sent(block, block, ah_sems, (i, j, k + 1), {"head": peer})
+                for j, peer in enumerate(head_peers)
+            ]
+
+    def late():
+        for copy in phase["group"]:
+            copy.wait_recv()
+        for held, total, everyone, place in (
+            (norm_held, norm_sum, norm_all, 0),
+            (shared_held, shared_sum, shared_all, 1),
+        ):
+            value = held[0]
+            for k in range(1, heads * tensors):
+                value = value + held[k]
+            total[...] = value
+            everyone[me] = value
+            phase["late", place] = [
+                sent(total, everyone.at[me], late_sems, (place, k), {"fsdp": other})
+                for k, other in enumerate(others)
+            ]
+
+    events = [
+        (0, start_a),
+        (1, lambda: to_b(0)), (1, lambda: to_b(1)),
+        (2, lambda: spread(0)), (3, lambda: spread(1)),
+        (4, lambda: forward(0)), (4, late), (5, lambda: forward(1)),
+    ]
+    ways = column_ways(g_ref.shape[2])
+    ring = [[] for _ in ways]
     for step in range(count - 1):
-        for way in (0, 1):
-            shift = 2 * count - 1 - step if way == 0 else 1 + step
+        for way, (start, amount) in enumerate(ways):
+            columns = pl.ds(start, amount)
+            shift = 2 * count - 1 - step if way % 2 == 0 else 1 + step
             block = ring_index((position + shift) % count, count)
+            held = slots[way]
             if step == 0:
-                source = g_ref.at[block, :, columns[way]]
+                source = g_ref.at[block, :, columns]
             else:
-                copies[way][step - 1].wait_recv()
-                held = slots[way]
+                ring[way][step - 1].wait_recv()
                 held[step - 1] = (
                     held[step - 1].astype(jnp.float32)
-                    + g_ref[block, :, columns[way]].astype(jnp.float32)
+                    + g_ref[block, :, columns].astype(jnp.float32)
                 ).astype(held.dtype)
                 source = held.at[step - 1]
-            copy = pltpu.make_async_remote_copy(
-                src_ref=source,
-                dst_ref=slots[way].at[step],
-                send_sem=send_sem.at[way, step],
-                recv_sem=recv_sem.at[way, step],
-                device_id={"fsdp": targets[way]},
-                device_id_type=MESH,
+            ring[way].append(
+                sent(source, held.at[step], ring_sems, (way, step), {"fsdp": targets[way % 2]})
             )
-            copy.start()
-            copies[way].append(copy)
-    for way in (0, 1):
-        copies[way][count - 2].wait_recv()
-        o_ref[:, columns[way]] = slots[way][count - 2].astype(jnp.float32) + g_ref[
-            me, :, columns[way]
+        while events and events[0][0] <= step:
+            events.pop(0)[1]()
+    for _, event in events:
+        event()
+    side = pl.ds(side_at, LANES)
+    order = sorted(
+        range(len(ways)), key=lambda way: not ways[way][0] <= side_at < ways[way][0] + ways[way][1]
+    )
+    for way in order:
+        start, amount = ways[way]
+        columns = pl.ds(start, amount)
+        ring[way][count - 2].wait_recv()
+        own_ref[:, columns] = slots[way][count - 2].astype(jnp.float32) + g_ref[
+            me, :, columns
         ].astype(jnp.float32)
-        for copy in copies[way]:
-            copy.wait_send()
-
-
-def ring_scatter(blocks):
-    count, rows, width = blocks.shape
-    split = (width // LANES + 1) // 2 * LANES
+        if start <= side_at < start + amount:
+            bc_ref[group_me] = own_ref[:, side]
+            bc_copies = [
+                sent(bc_ref.at[group_me], bc_ref.at[group_me], bc_sems, k, {"head": h, "tensor": t})
+                for k, (h, t) in enumerate(peers)
+            ]
+    for copies, everyone, total in (
+        (phase["lone"], lone_all, lone_out),
+        (phase["late", 0], norm_all, norm_out),
+        (phase["late", 1], shared_all, shared_out),
+    ):
+        for copy in copies:
+            copy.wait_recv()
+        value = everyone[0]
+        for k in range(1, count):
+            value = value + everyone[k]
+        total[...] = value
+    for i in range(2):
+        for copy in phase["h", i]:
+            copy.wait_recv()
+    for copy in bc_copies:
+        copy.wait_recv()
+    for copy in started:
+        copy.wait_send()
+
+
+def closing(grads, d_normed, partial_out, features, scale, gain, lone, shared, side_at):
+    count, heads, tensors = (lax.axis_size(a) for a in ("fsdp", "head", "tensor"))
+    size = heads * tensors
+    _, rows, columns = grads.shape
+    _, owned, width = d_normed.shape
+    low, full = grads.dtype, jnp.float32
+    ways = column_ways(columns)
+    assert all(amount > 0 for _, amount in ways)
+    dma = pltpu.SemaphoreType.DMA
+    shapes = [
+        (WAYS, count - 1), (2, heads - 1), (2, tensors - 1), (2, tensors - 1),
+        (2, heads - 1, tensors), (2, size - 1), (count - 1,), (2, count - 1), (size - 1,),
+    ]
     return pl.pallas_call(
-        partial(scatter_kernel, count, split),
-        out_shape=jax.ShapeDtypeStruct((rows, width), jnp.float32),
-        in_specs=[VMEM_SPEC],
-        out_specs=VMEM_SPEC,
-        scratch_shapes=[
-            pltpu.VMEM((count - 1, rows, split), blocks.dtype),
-            pltpu.VMEM((count - 1, rows, width - split), blocks.dtype),
-            pltpu.SemaphoreType.DMA((2, count - 1)),
-            pltpu.SemaphoreType.DMA((2, count - 1)),
+        partial(closing_kernel, count, heads, tensors, side_at),
+        out_shape=[
+            jax.ShapeDtypeStruct((rows, columns), full),
+            jax.ShapeDtypeStruct((size, owned, width), low),
+            jax.ShapeDtypeStruct((size, owned, width), low),
+            jax.ShapeDtypeStruct((size, rows, LANES), full),
+            jax.ShapeDtypeStruct(lone.shape, full),
+            jax.ShapeDtypeStruct(shared.shape, full),
+            jax.ShapeDtypeStruct((1, width), full),
         ],
+        in_specs=[VMEM_SPEC] * 8,
+        out_specs=[VMEM_SPEC] * 7,
+        scratch_shapes=[pltpu.VMEM((count - 1, rows, amount), low) for _, amount in ways]
+        + [
+            pltpu.VMEM((2, heads - 1, tensors, owned, width), low),
+            pltpu.VMEM((2, tensors, owned, width), low),
+            pltpu.VMEM((2, tensors - 1, owned, width), low),
+            pltpu.VMEM((1, width), full),
+            pltpu.VMEM((size, 1, width), full),
+            pltpu.VMEM((1, width), full),
+            pltpu.VMEM((size,) + shared.shape, full),
+            pltpu.VMEM(shared.shape, full),
+            pltpu.VMEM((count,) + lone.shape, full),
+            pltpu.VMEM((count,) + shared.shape, full),
+            pltpu.VMEM((count, 1, width), full),
+        ]
+        + [dma(shape) for shape in shapes for _ in range(2)],
         compiler_params=pltpu.CompilerParams(collective_id=1, has_side_effects=True),
-        name="ring_scatter",
-    )(blocks)
+        name="closing",
+    )(grads, d_normed, partial_out, features, scale, gain, lone, shared)
 
 
 def group_peers(heads, tensors):
@@ -216,34 +426,6 @@
         ],
         compiler_params=pltpu.CompilerParams(collective_id=collective, has_side_effects=True),
         name=f"group_sum_{collective}",
-    )(x)
-
-
-def group_gather_kernel(heads, tensors, x_ref, o_ref, send_sem, recv_sem):
-    me, peers = group_peers(heads, tensors)
-    group_barrier(peers)
-    copies = group_exchange(peers, lambda head, tensor: x_ref, o_ref.at[me], send_sem, recv_sem)
-    o_ref[me] = x_ref[...]
-    for copy in copies:
-        copy.wait_recv()
-    for copy in copies:
-        copy.wait_send()
-
-
-def group_gather(x, collective):
-    heads, tensors = lax.axis_size("head"), lax.axis_size("tensor")
-    size = heads * tensors
-    return pl.pallas_call(
-        partial(group_gather_kernel, heads, tensors),
-        out_shape=jax.ShapeDtypeStruct((size,) + x.shape, x.dtype),
-        in_specs=[VMEM_SPEC],
-        out_specs=VMEM_SPEC,
-        scratch_shapes=[
-            pltpu.SemaphoreType.DMA((size - 1,)),
-            pltpu.SemaphoreType.DMA((size - 1,)),
-        ],
-        compiler_params=pltpu.CompilerParams(collective_id=collective, has_side_effects=True),
-        name=f"group_gather_{collective}",
     )(x)
 
 
@@ -424,6 +606,10 @@
     return a if extra == 0 else jnp.pad(a, ((0, 0),) * (a.ndim - 1) + ((0, extra),))
 
 
+def as_rows(flat):
+    return jnp.pad(flat, (0, -flat.shape[0] % (8 * LANES))).reshape(-1, LANES)
+
+
 def on_device(
     block_in, cotangent, norm_gain, w_x, w_z, w_bc, w_dt, conv_x, conv_bc, dt_bias, a_log, skip,
     gate_gain, w_out,
@@ -503,10 +689,6 @@
     normed_out = (gated * scale_out * gain).astype(jnp.bfloat16)
     partial_out = last_axes(normed_out, weight_out).astype(jnp.bfloat16)
     mine = lambda a: lax.dynamic_slice_in_dim(a, group_at * owned, owned, 0)
-    summed = group_sum(partial_out.reshape(size, owned, width), True, 3)
-    own_out = (summed + mine(features)).astype(jnp.bfloat16)
-    block_out = group_gather(own_out, 4).reshape(length, width)
-
     g_gate_gain = jnp.sum(d_normed_out * gated * scale_out, axis=0)
     d_gated = scale_out * d_hat - gated * scale_out**3 * (inner_sum / full_inner)
     d_mixed = d_gated * z_silu
@@ -561,16 +743,6 @@
     local_part = last_axes(d_cat[:, : 2 * inner], weights[:, : 2 * inner]) + last_axes(
         d_cat[:, 2 * inner :], side
     )
-    d_normed = group_sum(local_part.astype(jnp.bfloat16).reshape(size, owned, width), True, 6)
-    own_features, own_scale = mine(features), mine(scale_in)
-    g_norm_gain = jnp.sum(d_normed * own_features * own_scale, axis=0)
-    d_in_hat = d_normed * norm_gain
-    own_grad = own_scale * d_in_hat - own_features * own_scale**3 * jnp.mean(
-        d_in_hat * own_features, axis=1, keepdims=True
-    )
-    others = group_gather(own_grad.astype(jnp.bfloat16), 7).reshape(length, width)
-    grad_in = others.astype(jnp.float32) + cotangent.astype(jnp.float32)
-
     grads = jnp.concatenate(
         [
             first_axes(normed, d_cat).astype(jnp.bfloat16),
@@ -578,52 +750,49 @@
         ],
         axis=1,
     )
-    own = ring_scatter(grads.reshape(count, rows, grads.shape[1]))
-    side_at = 2 * inner
-    g_w_bc = group_gather(pad_lanes(own[:, side_at : side_at + quarter]), 8)[:, :, :quarter]
-    g_w_bc = g_w_bc.transpose(1, 0, 2).reshape(rows, 2, state)
-
-    small = lax.psum(
-        jnp.concatenate(
-            [g_norm_gain, g_conv_x.reshape(-1), g_gate_gain, g_conv_bc.reshape(-1), g_dt_bias, g_a_log, g_skip]
-        ),
-        "fsdp",
-    )
-    cuts = []
-    start = 0
-    for amount in (width, taps * inner, inner, taps * quarter, head_count, head_count, head_count):
-        cuts.append(small[start : start + amount])
-        start += amount
+    lone = as_rows(jnp.concatenate([g_conv_x.reshape(-1), g_gate_gain, g_dt_bias]))
     spread = jnp.zeros((2 * state, taps), jnp.float32)
-    spread = lax.dynamic_update_slice_in_dim(
-        spread, cuts[3].reshape(taps, quarter).T, group_at * quarter, 0
-    )
+    spread = lax.dynamic_update_slice_in_dim(spread, g_conv_bc.T, group_at * quarter, 0)
     by_head = jnp.zeros((heads, 2 * head_count), jnp.float32)
     by_head = lax.dynamic_update_slice_in_dim(
-        by_head, jnp.concatenate([cuts[5], cuts[6]])[None], head_at, 0
-    )
-    last = jnp.concatenate([cuts[0], spread.reshape(-1), by_head.reshape(-1)])
-    total = last.shape[0]
-    last = jnp.pad(last, (0, -total % (8 * LANES))).reshape(-1, LANES)
-    last = group_sum(last, False, 9).reshape(-1)
-    at_heads = width + 2 * state * taps
-    mine_head = lax.dynamic_slice_in_dim(
-        last[at_heads:total].reshape(heads, 2 * head_count), head_at, 1, 0
+        by_head, jnp.concatenate([g_a_log, g_skip])[None], head_at, 0
+    )
+    shared = as_rows(jnp.concatenate([spread.reshape(-1), by_head.reshape(-1)]))
+    side_at = 2 * inner
+    own, out_all, grad_all, bc_all, lone, shared, g_norm_gain = closing(
+        grads.reshape(count, rows, grads.shape[1]),
+        local_part.astype(jnp.bfloat16).reshape(size, owned, width),
+        partial_out.reshape(size, owned, width),
+        mine(features),
+        mine(scale_in),
+        norm_gain[None, :],
+        lone,
+        shared,
+        side_at,
+    )
+    block_out = out_all.reshape(length, width)
+    grad_in = grad_all.reshape(length, width).astype(jnp.float32) + cotangent.astype(jnp.float32)
+    g_w_bc = bc_all[:, :, :quarter].transpose(1, 0, 2).reshape(rows, 2, state)
+    lone, shared = lone.reshape(-1), shared.reshape(-1)
+    at_heads = 2 * state * taps
+    by_head = lax.dynamic_slice_in_dim(
+        shared[at_heads : at_heads + 2 * head_count * heads].reshape(heads, 2 * head_count), head_at, 1, 0
     )[0]
+    wide = taps * inner
     return (
         block_out,
         grad_in,
-        last[:width],
+        g_norm_gain.reshape(width),
         own[:, :inner].reshape(rows, head_count, head_width),
         own[:, inner : 2 * inner].reshape(rows, head_count, head_width),
         g_w_bc,
         own[:, side_at + quarter : side_at + quarter + head_count],
-        cuts[1].reshape(taps, inner).T.reshape(head_count, head_width, taps),
-        last[width:at_heads].reshape(2, state, taps),
-        cuts[4],
-        mine_head[:head_count],
-        mine_head[head_count:],
-        cuts[2].reshape(head_count, head_width),
+        lone[:wide].reshape(taps, inner).T.reshape(head_count, head_width, taps),
+        shared[:at_heads].reshape(2, state, taps),
+        lone[wide + inner : wide + inner + head_count],
+        by_head[:head_count],
+        by_head[head_count:],
+        lone[wide : wide + inner].reshape(head_count, head_width),
         own[:, own.shape[1] - inner :].T.reshape(head_count, head_width, rows),
     )
 

time: 344 us -> 220 us (0.64)
  Pallas kernels: 224 us -> 146 us
  blocking collectives: 35.7 us -> 0 us
  local copies, waits for them, and re-layouts: 35.4 us -> 28.8 us
    pallas_call x5 -> x2, Pallas kernels: 141 us -> 98.9 us  [the longest x1 51.9 us: closing(): pl.pallas_call(partial(closing_kernel, count, heads, tensors, side_at), o...]
    pallas_call x5 -> x2, Pallas kernels: 51.6 us -> 14.8 us  [group_sum(): pl.pallas_call(partial(group_sum_kernel, heads, tensors, scattered), out_...]
    psum x1 -> x0, blocking collectives: 35.7 us -> none  [on_device(): lax.psum(jnp.concatenate([g_norm_gain, g_conv_x.reshape(-1), g_gate_gain,...]
    unnamed x60 -> x75, local copies, waits for them, and re-layouts: 9.8 us -> 9.14 us
where the time goes in v2:
time: 220 us; the launch traced here: 219 us
  Pallas kernels  146 us (66%)
  local copies, waits for them, and re-layouts  28.8 us (13%)
  other arithmetic  23.1 us (10%)
  matrix products  20.2 us (9%)
    pallas_call x1, Pallas kernels, closing(): pl.pallas_call(partial(closing_kernel, count, heads, tensors, side_at), o...  51.9 us
    pallas_call x1, Pallas kernels, ring_gather(): pl.pallas_call(partial(gather_kernel, count), out_shape=jax.ShapeDtypeStr...  47 us
    pallas_call x1, Pallas kernels, mix_back(): pl.pallas_call(partial(back_kernel, per, width), grid=(groups,), in_specs...  21 us
    pallas_call x2, Pallas kernels, group_sum(): pl.pallas_call(partial(group_sum_kernel, heads, tensors, scattered), out_...  14.8 us
    pallas_call x1, Pallas kernels, mix(): pl.pallas_call(partial(mix_kernel, per, width), grid=(inner // (per * wid...  10.9 us
    unnamed x75, local copies, waits for them, and re-layouts  9.14 us
    dot_general x3, matrix products, last_axes(): lax.dot_general(a, b, (((1,), (1,)), ((), ())), preferred_element_type=jn...  7.44 us
    dot_general x1, matrix products, on_device(): jnp.dot(cotangent, weight_out, preferred_element_type=jnp.float32)  4.49 us

profile of v2, /device:TPU:0, one launch (start us, length us, event | category | flops | bytes accessed | tf_op | source)
XLA Modules:
  0.0 219.0 jit_solution(17105340721825730655)
XLA Ops:
  0.6 1.0 copy.96
  1.7 1.0 copy.97
  2.7 0.9 bitcast_dynamic-update-slice_fusion.1
  4.4 1.0 copy.95
  6.2 47.0 %ring_gather.1 = bf16[8,128,1920]{2,1,0:T(8,128)(2,1)} custom-call(bf16[128,1920]{1,0:T(8,128)(2,1)} %copy-done.13), custom_call_target="tpu_custom_call" | custom-call | tf_op jit(solution)/shard_map/ring_gather/pallas_call | solution.py:87
  53.6 3.7 %fusion = f32[512,1408]{1,0:T(8,128)S(1)} fusion(bf16[1024,1920]{1,0:T(8,128)(2,1)} %bitcast.116, f32[1024]{0:T(1024)S(1)} %copy-done.26, f32[512]{0:T(512)S(1)} %add_rsqrt_fusion, bf16[512,1024]{1,0:T(8,128)(2,1)S(1)} %copy-done.4), kind=kOutput, calls=%fused_computation.2 | convolution fusion | flops 1478492160 | bytes 6821888 | tf_op jit(solution)/shard_map/dot_general | solution.py:647
  57.3 1.6 copy-done.3
  59.8 1.8 multiply_convert_fusion.3
  61.5 1.1 slice.270
  63.7 1.1 compare_select_fusion
  65.4 1.5 copy.102
  67.6 1.3 copy.101
  68.9 10.9 %mix.1.y_ref = f32[512,512]{1,0:T(8,128)} custom-call(bf16[512,128]{1,0:T(8,128)(2,1)} %get-tuple-element.120.b_ref, bf16[512,128]{1,0:T(8,128)(2,1)} %get-tuple-element.119.c_ref, bf16[512,512]{1,0:T(8,128)(2,1)} %get-tuple-element.111.x_ref, f32[4,512,4]{2,1,0:T(8,128)} %bitcast.114, f32[4,512,4]{2,1,0:T(8,128)} %bitcast.112, f32[4,4,512]{2,1,0:T(4,128)} %reshape.222.row_ref), custom_call_target="tpu_custom_call" | custom-call | tf_op jit(solution)/shard_map/mix/pallas_call | solution.py:535
  80.0 4.5 %multiply_reduce_fusion.7 = (f32[512]{0:T(512)S(1)}, f32[512]{0:T(512)S(1)}, f32[512,512]{1,0:T(8,128)}, f32[512,512]{1,0:T(8,128)}) fusion(f32[512]{0:T(512)S(1)} %mul.429, f32[512,1408]{1,0:T(8,128)} %copy-done.3, f32[512,512]{1,0:T(8,128)} %mix.1.y_ref, bf16[512,512]{1,0:T(8,128)(2,1)S(1)} %copy-done.1, f32[512]{0:T(512)S(1)} %mul.423, ...), kind=kOutput, calls=%fused_computation.49 | convolution fusion | flops 540277760 | bytes 6823936 | tf_op jit(solution)/shard_map/dot_general | solution.py:683
  85.1 4.9 %group_sum_2.1 = f32[8,128]{1,0:T(8,128)} custom-call(f32[8,128]{1,0:T(8,128)} %pad_maximum_fusion.6.x_ref), custom_call_target="tpu_custom_call" | custom-call | tf_op jit(solution)/shard_map/group_sum_2/pallas_call | solution.py:417
  91.6 3.9 %fusion.18 = (f32[512]{0:T(512)S(1)}, f32[512,512]{1,0:T(8,128)}, bf16[512,512]{1,0:T(8,128)(2,1)}, f32[512]{0:T(512)S(1)}) fusion(bf16[512,512]{1,0:T(8,128)(2,1)S(1)} %copy-done.1, f32[512,1408]{1,0:T(8,128)} %copy-done.3, f32[512]{0:T(512)S(1)} %get-tuple-element.133, f32[512,512]{1,0:T(8,128)} %get-tuple-element.110, f32[512]{0:T(512)S(1)} %multiply_multiply_fusion.2, ...), kind=kLoop, calls=%fused_computation.35 | loop fusion | flops 6552576 | bytes 6305792 | tf_op jit(solution)/shard_map/reduce_sum | solution.py:703
  96.2 21.0 %mix_back.1 = (f32[512,512]{1,0:T(8,128)}, f32[4,512,4]{2,1,0:T(8,128)}, f32[4,512,4]{2,1,0:T(8,128)}, f32[512,128]{1,0:T(8,128)}, f32[512,128]{1,0:T(8,128)}) custom-call(bf16[512,128]{1,0:T(8,128)(2,1)} %get-tuple-element.120.b_ref, bf16[512,128]{1,0:T(8,128)(2,1)} %get-tuple-element.119.c_ref, bf16[512,512]{1,0:T(8,128)(2,1)} %get-tuple-element.111.x_ref, ...), custom_call_target="tpu_custom_call" | custom-call | tf_op jit(solution)/shard_map/mix_back/pallas_call | solution.py:551
  117.2 1.7 copy.104
  119.4 1.6 multiply_convert_fusion.8
  121.7 0.9 pad_maximum_fusion.1.x_ref
  122.6 9.9 %group_sum_5.1 = f32[512,128]{1,0:T(8,128)} custom-call(bf16[4,512,128]{2,1,0:T(8,128)(2,1)} %pad_maximum_fusion.1.x_ref), custom_call_target="tpu_custom_call" | custom-call | tf_op jit(solution)/shard_map/group_sum_5/pallas_call | solution.py:417
  132.7 1.3 multiply_reduce_fusion.12
  135.5 2.5 %multiply_reduce_fusion.5 = (f32[512]{0:T(512)S(1)}, f32[512]{0:T(512)S(1)}, f32[512]{0:T(512)S(1)}, f32[512]{0:T(512)S(1)}, f32[512,512]{1,0:T(8,128)S(1)}) fusion(f32[512,512]{1,0:T(8,128)S(1)} %slice.277, f32[512,1408]{1,0:T(8,128)} %copy-done.3, f32[512,512]{1,0:T(8,128)} %get-tuple-element.26, f32[512,512]{1,0:T(8,128)S(1)} %copy-done.7), kind=kLoop, calls=%fused_computation.43 | loop fusion | flops 4192256 | bytes 5251072 | tf_op jit(solution)/shard_map/reduce_sum | solution.py:599
  138.8 1.7 convolution_convert_fusion.1
  141.0 2.6 %fusion.2 = f32[512,1024]{1,0:T(8,128)} fusion(bf16[1024,1920]{1,0:T(8,128)(2,1)S(1)} %bitcast.120, bf16[512,512]{1,0:T(8,128)(2,1)S(1)} %copy-done.14, bf16[512,512]{1,0:T(8,128)(2,1)S(1)} %fusion.14), kind=kOutput, calls=%fused_computation.4 | convolution fusion | flops 1075838976 | bytes 5242880 | tf_op jit(solution)/shard_map/dot_general | solution.py:440
  144.3 1.1 slice_multiply_fusion
  145.4 3.1 %add_convert_fusion = bf16[512,1024]{1,0:T(8,128)(2,1)} fusion(f32[512,1024]{1,0:T(8,128)} %fusion.2, bf16[512,128]{1,0:T(8,128)(2,1)S(1)} %fusion.55, bf16[1024,16]{1,0:T(8,128)(2,1)S(1)} %slice_multiply_fusion, bf16[1024,64]{1,0:T(8,128)(2,1)S(1)} %constant_dynamic-slice_fusion.2), kind=kOutput, calls=%fused_computation.7 | convolution fusion | flops 136183808 | bytes 3440640 | tf_op jit(solution)/shard_map/dot_general | solution.py:440
  148.5 1.7 convolution_convert_fusion
  151.0 2.0 pad_maximum_fusion
  154.9 51.9 %closing.1 = (f32[128,1664]{1,0:T(8,128)}, bf16[4,128,1024]{2,1,0:T(8,128)(2,1)}, bf16[4,128,1024]{2,1,0:T(8,128)(2,1)}, f32[4,128,128]{2,1,0:T(8,128)}, f32[24,...) custom-call(bf16[8,128,1664]{2,1,0:T(8,128)(2,1)} %bitcast.111, bf16[4,128,1024]{2,1,0:T(8,128)(2,1)} %bitcast.122, ...), custom_call_target="tpu_custom_call" | custom-call | tf_op jit(solution)/shard_map/closing/pallas_call | solution.py:326
  206.7 3.0 %convert_add_fusion = f32[512,1024]{1,0:T(8,128)} fusion(bf16[512,1024]{1,0:T(8,128)(2,1)S(1)} %copy-done.8, bf16[4,128,1024]{2,1,0:T(8,128)(2,1)} %get-tuple-element.32), kind=kLoop, calls=%fused_computation.6 | loop fusion | flops 1572864 | bytes 4194304 | tf_op jit(solution)/shard_map/add | solution.py:774
  217.5 1.0 copy.134
  (156 shorter events, 23.6 us)
Async XLA Ops:
  5.4 0.8 copy-start.13
  6.2 47.0 %copy-start.4 = (bf16[512,1024]{1,0:T(8,128)(2,1)S(1)}, bf16[512,1024]{1,0:T(8,128)(2,1)}, u32[]{:S(2)}) copy-start(bf16[512,1024]{1,0:T(8,128)(2,1)} %param.14) | copy-start | bytes 3145732
  6.2 47.3 %copy-start.26 = (f32[1024]{0:T(1024)S(1)}, f32[1024]{0:T(1024)}, u32[]{:S(2)}) copy-start(f32[1024]{0:T(1024)} %param.16) | copy-start | bytes 12292
  57.3 1.6 copy-start.3
  58.9 0.8 copy-start.21
  59.6 3.0 %copy-start.23 = (f32[2,128,4]{1,2,0:T(4,128)S(1)}, f32[2,128,4]{1,2,0:T(4,128)}, u32[]{:S(2)}) copy-start(f32[2,128,4]{1,2,0:T(4,128)} %param.22) | copy-start | bytes 12292
  59.7 4.0 %copy-start.28 = (f32[16]{0:T(128)S(1)}, f32[16]{0:T(128)}, u32[]{:S(2)}) copy-start(f32[16]{0:T(128)} %param.23) | copy-start | bytes 196
  61.5 3.3 %copy-start.30 = (f32[16]{0:T(128)S(1)}, f32[16]{0:T(128)}, u32[]{:S(2)}) copy-start(f32[16]{0:T(128)} %param.24) | copy-start | bytes 196
  68.9 10.9 %copy-start.25 = (f32[16,32]{1,0:T(8,128)S(1)}, f32[16,32]{1,0:T(8,128)}, u32[]{:S(2)}) copy-start(f32[16,32]{1,0:T(8,128)} %param.26) | copy-start | bytes 6148
  68.9 11.0 %copy-start.29 = (f32[16]{0:T(128)S(1)}, f32[16]{0:T(128)}, u32[]{:S(2)}) copy-start(f32[16]{0:T(128)} %param.25) | copy-start | bytes 196
  68.9 11.1 %copy-start.1 = (bf16[512,512]{1,0:T(8,128)(2,1)S(1)}, bf16[512,512]{1,0:T(8,128)(2,1)}, u32[]{:S(2)}) copy-start(bf16[512,512]{1,0:T(8,128)(2,1)} %get-tuple-element.111.x_ref) | copy-start | bytes 1572868
  80.0 11.5 %copy-start = (f32[512,512]{1,0:T(8,128)S(1)}, f32[512,512]{1,0:T(8,128)}, u32[]{:S(2)}) copy-start(f32[512,512]{1,0:T(8,128)} %mix.1.y_ref) | copy-start | bytes 3145732
  117.1 1.8 copy-start.11
  117.1 3.8 %copy-start.19 = (f32[512,128]{1,0:T(8,128)S(1)}, f32[512,128]{1,0:T(8,128)}, u32[]{:S(2)}) copy-start(f32[512,128]{1,0:T(8,128)} %get-tuple-element.27) | copy-start | bytes 786436
  119.4 2.0 copy-start.18
  121.6 13.9 %copy-start.7 = (f32[512,512]{1,0:T(8,128)S(1)}, f32[512,512]{1,0:T(8,128)}, u32[]{:S(2)}) copy-start(f32[512,512]{1,0:T(8,128)} %get-tuple-element.112) | copy-start | bytes 3145732
  135.5 2.5 %copy-start.9 = (f32[512,128]{1,0:T(8,128)S(1)}, f32[512,128]{1,0:T(8,128)}, u32[]{:S(2)}) copy-start(f32[512,128]{1,0:T(8,128)} %group_sum_5.1) | copy-start | bytes 786436
  135.5 3.3 %copy-start.2 = (bf16[8,128,1920]{2,1,0:T(8,128)(2,1)S(1)}, bf16[8,128,1920]{2,1,0:T(8,128)(2,1)}, u32[]{:S(2)}) copy-start(bf16[8,128,1920]{2,1,0:T(8,128)(2,1)} %ring_gather.1) | copy-start | bytes 11796484
  135.5 3.3 %copy-start.6 = (f32[512,512]{1,0:T(8,128)S(1)}, f32[512,512]{1,0:T(8,128)}, u32[]{:S(2)}) copy-start(f32[512,512]{1,0:T(8,128)} %get-tuple-element.110) | copy-start | bytes 3145732
  138.8 2.2 %copy-start.14 = (bf16[512,512]{1,0:T(8,128)(2,1)S(1)}, bf16[512,512]{1,0:T(8,128)(2,1)}, u32[]{:S(2)}) copy-start(bf16[512,512]{1,0:T(8,128)(2,1)} %get-tuple-element.113) | copy-start | bytes 1572868
  141.0 2.6 %copy-start.16 = (bf16[512,512]{1,0:T(8,128)(2,1)}, bf16[512,512]{1,0:T(8,128)(2,1)S(1)}, u32[]{:S(2)}) copy-start(bf16[512,512]{1,0:T(8,128)(2,1)S(1)} %fusion.14) | copy-start | bytes 1572868
  144.2 4.2 %copy-start.5 = (bf16[512,1024]{1,0:T(8,128)(2,1)S(1)}, bf16[512,1024]{1,0:T(8,128)(2,1)}, u32[]{:S(2)}) copy-start(bf16[512,1024]{1,0:T(8,128)(2,1)} %param.14) | copy-start | bytes 3145732
  144.2 4.2 %copy-start.15 = (bf16[512,512]{1,0:T(8,128)(2,1)S(1)}, bf16[512,512]{1,0:T(8,128)(2,1)}, u32[]{:S(2)}) copy-start(bf16[512,512]{1,0:T(8,128)(2,1)} %get-tuple-element.113) | copy-start | bytes 1572868
  144.2 4.2 %copy-start.17 = (bf16[512,512]{1,0:T(8,128)(2,1)S(1)}, bf16[512,512]{1,0:T(8,128)(2,1)}, u32[]{:S(2)}) copy-start(bf16[512,512]{1,0:T(8,128)(2,1)} %copy-done.16) | copy-start | bytes 1572868
  148.5 1.7 copy-start.8
  206.7 3.0 %copy-start.12 = (f32[128,1664]{1,0:T(8,128)S(1)}, f32[128,1664]{1,0:T(8,128)}, u32[]{:S(2)}) copy-start(f32[128,1664]{1,0:T(8,128)} %get-tuple-element.34) | copy-start | bytes 2555908
  209.7 2.6 %copy-start.20 = (f32[4,128,128]{2,1,0:T(8,128)S(1)}, f32[4,128,128]{2,1,0:T(8,128)}, u32[]{:S(2)}) copy-start(f32[4,128,128]{2,1,0:T(8,128)} %get-tuple-element.35) | copy-start | bytes 786436
  209.7 3.5 %copy-start.22 = (f32[16,128]{1,0:T(8,128)S(1)}, f32[16,128]{1,0:T(8,128)}, u32[]{:S(2)}) copy-start(f32[16,128]{1,0:T(8,128)} %get-tuple-element.37) | copy-start | bytes 24580
  209.8 4.3 %copy-start.24 = (f32[24,128]{1,0:T(8,128)S(1)}, f32[24,128]{1,0:T(8,128)}, u32[]{:S(2)}) copy-start(f32[24,128]{1,0:T(8,128)} %get-tuple-element.36) | copy-start | bytes 36868
  209.9 7.6 %copy-start.10 = (bf16[4,128,1024]{2,1,0:T(8,128)(2,1)S(1)}, bf16[4,128,1024]{2,1,0:T(8,128)(2,1)}, u32[]{:S(2)}) copy-start(bf16[4,128,1024]{2,1,0:T(8,128)(2,1)} %get-tuple-element.31) | copy-start | bytes 3145732
  212.4 6.1 %copy-start.27 = (f32[1,1024]{1,0:T(1,128)S(1)}, f32[1,1024]{1,0:T(1,128)}, u32[]{:S(2)}) copy-start(f32[1,1024]{1,0:T(1,128)} %get-tuple-element.33) | copy-start | bytes 12292

commit v3 on v2

--- a/solution.py
+++ b/solution.py
@@ -11,7 +11,7 @@
 PRECISE = lax.Precision.HIGHEST
 LANES = 128
 CHUNK = 256
-WAYS = 4
+WAYS = 6
 MESH = pl.DeviceIdType.MESH
 VMEM_SPEC = pl.BlockSpec(memory_space=pltpu.VMEM)
 
@@ -444,7 +444,7 @@
     return lax.dot_general(a, b, (((0,), (0,)), ((), ())), preferred_element_type=jnp.float32)
 
 
-def mix_kernel(per, width, b_ref, c_ref, x_ref, step_ref, col_ref, row_ref, y_ref, scores):
+def mix_kernel(per, width, b_ref, c_ref, x_ref, row_ref, y_ref, scores):
     length = x_ref.shape[0]
     chunk = min(CHUNK, length)
 
@@ -452,15 +452,16 @@
     def _():
         scores[...] = last_axes(c_ref[...], b_ref[...])
 
+    columns = row_ref[0].T
     for head in range(per):
         part = slice(head * width, (head + 1) * width)
-        step = step_ref[0, :, head : head + 1]
+        step = columns[:, head : head + 1]
         v = (x_ref[:, part].astype(jnp.float32) * step).astype(jnp.bfloat16)
         for first in range(0, length, chunk):
             seen = first + chunk
             decay = decay_tile(
-                col_ref[0, first:seen, head : head + 1],
-                row_ref[0, head : head + 1, :seen],
+                columns[first:seen, per + head : per + head + 1],
+                row_ref[0, per + head : per + head + 1, :seen],
                 first,
                 chunk,
                 seen,
@@ -470,8 +471,8 @@
 
 
 def back_kernel(
-    per, width, b_ref, c_ref, x_ref, dy_ref, y_ref, skip_ref, step_ref, col_ref, row_ref,
-    dx_ref, dstep_ref, dcums_ref, db_ref, dc_ref, scores, d_scores, carried,
+    per, width, b_ref, c_ref, x_ref, dy_ref, y_ref, skip_ref, row_ref,
+    dx_ref, drow_ref, db_ref, dc_ref, scores, d_scores, carried, side, low_v, low_dy,
 ):
     length = x_ref.shape[0]
     chunk = min(CHUNK, length)
@@ -481,34 +482,43 @@
         scores[...] = last_axes(c_ref[...], b_ref[...])
         d_scores[...] = jnp.zeros_like(d_scores)
 
+    columns = row_ref[0].T
     for head in range(per):
         part = slice(head * width, (head + 1) * width)
-        step = step_ref[0, :, head : head + 1]
+        step = columns[:, head : head + 1]
         x = x_ref[:, part].astype(jnp.float32)
         v = (x * step).astype(jnp.bfloat16)
-        dy = dy_ref[:, part]
-        dy_low = dy.astype(jnp.bfloat16)
-        carried[...] = jnp.zeros_like(carried)
+        dy_low = dy_ref[:, part].astype(jnp.bfloat16)
+        low_v[:, part] = v
+        low_dy[:, part] = dy_low
+        carried[part] = jnp.zeros((width, length), jnp.float32)
         for first in range(0, length, chunk):
             seen = first + chunk
             decay = decay_tile(
-                col_ref[0, first:seen, head : head + 1],
-                row_ref[0, head : head + 1, :seen],
+                columns[first:seen, per + head : per + head + 1],
+                row_ref[0, per + head : per + head + 1, :seen],
                 first,
                 chunk,
                 seen,
             )
             a = (scores[first:seen, :seen] * decay).astype(jnp.bfloat16)
-            carried[:seen] += first_axes(a, dy_low[first:seen])
+            carried[part, :seen] += first_axes(dy_low[first:seen], a)
             d_scores[first:seen, :seen] += last_axes(dy_low[first:seen], v[:seen]) * decay
-        u = carried[...]
-        dx_ref[:, part] = step * u + skip_ref[:, part] * dy
-        dstep_ref[0, :, head : head + 1] = jnp.sum(x * u, axis=1, keepdims=True)
-        dcums_ref[0, :, head : head + 1] = jnp.sum(
-            dy_low.astype(jnp.float32) * y_ref[:, part] - v.astype(jnp.float32) * u,
-            axis=1,
-            keepdims=True,
+
+    u_all = carried[...].T
+    for head in range(per):
+        part = slice(head * width, (head + 1) * width)
+        step = columns[:, head : head + 1]
+        x = x_ref[:, part].astype(jnp.float32)
+        v = low_v[:, part].astype(jnp.float32)
+        dy_low = low_dy[:, part].astype(jnp.float32)
+        u = u_all[:, part]
+        dx_ref[:, part] = step * u + skip_ref[:, part] * dy_ref[:, part]
+        side[:, head : head + 1] = jnp.sum(x * u, axis=1, keepdims=True)
+        side[:, per + head : per + head + 1] = jnp.sum(
+            dy_low * y_ref[:, part] - v * u, axis=1, keepdims=True
         )
+    drow_ref[0] = side[...].T[: 2 * per]
 
     @pl.when(pl.program_id(0) == pl.num_programs(0) - 1)
     def _():
@@ -523,54 +533,55 @@
 
 def head_specs(length, per, width, state):
     wide = pl.BlockSpec((length, per * width), lambda i: (0, i))
-    col = pl.BlockSpec((1, length, per), lambda i: (i, 0, 0))
-    row = pl.BlockSpec((1, per, length), lambda i: (i, 0, 0))
-    return whole((length, state)), wide, col, row
-
-
-def mix(b, c, x, step, col, row, width):
+    row = pl.BlockSpec((1, 2 * per, length), lambda i: (i, 0, 0))
+    return whole((length, state)), wide, row
+
+
+def mix(b, c, x, row, width):
     length, inner = x.shape
-    per = col.shape[2]
-    maps, wide, col_spec, row_spec = head_specs(length, per, width, b.shape[1])
+    per = row.shape[1] // 2
+    maps, wide, row_spec = head_specs(length, per, width, b.shape[1])
     return pl.pallas_call(
         partial(mix_kernel, per, width),
         grid=(inner // (per * width),),
-        in_specs=[maps, maps, wide, col_spec, col_spec, row_spec],
+        in_specs=[maps, maps, wide, row_spec],
         out_specs=wide,
         out_shape=jax.ShapeDtypeStruct((length, inner), jnp.float32),
         scratch_shapes=[pltpu.VMEM((length, length), jnp.float32)],
         name="mix",
-    )(b, c, x, step, col, row)
-
-
-def mix_back(b, c, x, dy, y, skip_row, step, col, row, width):
+    )(b, c, x, row)
+
+
+def mix_back(b, c, x, dy, y, skip_row, row, width):
     length, inner = x.shape
-    groups, _, per = col.shape
+    groups, per = row.shape[0], row.shape[1] // 2
     state = b.shape[1]
-    maps, wide, col_spec, row_spec = head_specs(length, per, width, state)
+    maps, wide, row_spec = head_specs(length, per, width, state)
     return pl.pallas_call(
         partial(back_kernel, per, width),
         grid=(groups,),
         in_specs=[
             maps, maps, wide, wide, wide,
             pl.BlockSpec((1, per * width), lambda i: (0, i)),
-            col_spec, col_spec, row_spec,
+            row_spec,
         ],
-        out_specs=[wide, col_spec, col_spec, maps, maps],
+        out_specs=[wide, row_spec, maps, maps],
         out_shape=[
             jax.ShapeDtypeStruct((length, inner), jnp.float32),
-            jax.ShapeDtypeStruct((groups, length, per), jnp.float32),
-            jax.ShapeDtypeStruct((groups, length, per), jnp.float32),
+            jax.ShapeDtypeStruct(row.shape, jnp.float32),
             jax.ShapeDtypeStruct((length, state), jnp.float32),
             jax.ShapeDtypeStruct((length, state), jnp.float32),
         ],
         scratch_shapes=[
             pltpu.VMEM((length, length), jnp.float32),
             pltpu.VMEM((length, length), jnp.float32),
-            pltpu.VMEM((length, width), jnp.float32),
+            pltpu.VMEM((per * width, length), jnp.float32),
+            pltpu.VMEM((length, LANES), jnp.float32),
+            pltpu.VMEM((length, per * width), jnp.bfloat16),
+            pltpu.VMEM((length, per * width), jnp.bfloat16),
         ],
         name="mix_back",
-    )(b, c, x, dy, y, skip_row, step, col, row)
+    )(b, c, x, dy, y, skip_row, row)
 
 
 def delayed(signal, count):
@@ -648,7 +659,7 @@
     x_raw = raw[:, :inner]
     z_raw = raw[:, inner : 2 * inner]
     bc_raw = raw[:, 2 * inner : dt_at]
-    dt_in = raw[:, dt_at : dt_at + head_count] + dt_bias
+    dt_in = raw[:, dt_at : dt_at + head_count].T + dt_bias[:, None]
     kernel_x = conv_x.reshape(inner, taps)
     kernel_bc = conv_bc.reshape(2 * state, taps)
     gain = gate_gain.reshape(inner)
@@ -662,18 +673,10 @@
     rate = -jnp.exp(a_log)
     at = jnp.arange(length)
     lower = (at[:, None] >= at[None, :]).astype(jnp.float32)
-    cums = jnp.dot(lower, step * rate, precision=PRECISE)
-
-    def as_columns(a):
-        return a.reshape(length, head_count // per, per).transpose(1, 0, 2)
-
-    def from_columns(a):
-        return a.transpose(1, 0, 2).reshape(length, head_count)
-
-    step_col = as_columns(step)
-    col = as_columns(cums)
-    row = cums.T.reshape(head_count // per, per, length)
-    scanned = mix(b_maps, c_maps, x_act, step_col, col, row, head_width)
+    cums = jnp.dot(step * rate[:, None], lower.T, precision=PRECISE)
+    by_group = (head_count // per, per, length)
+    row = jnp.concatenate([step.reshape(by_group), cums.reshape(by_group)], axis=1)
+    scanned = mix(b_maps, c_maps, x_act, row, head_width)
     skip_row = jnp.repeat(skip, head_width)[None, :]
     x_wide = x_act.astype(jnp.float32)
     mixed = scanned + skip_row * x_wide
@@ -693,13 +696,13 @@
     d_gated = scale_out * d_hat - gated * scale_out**3 * (inner_sum / full_inner)
     d_mixed = d_gated * z_silu
     d_z = (d_gated * mixed * (z_sigma * (1.0 + z_raw * (1.0 - z_sigma)))).astype(jnp.bfloat16)
-    d_xs, d_step, d_cums, d_b, d_c = mix_back(
-        b_maps, c_maps, x_act, d_mixed, scanned, skip_row, step_col, col, row, head_width
-    )
-    d_logs = jnp.dot(lower.T, from_columns(d_cums), precision=PRECISE)
-    d_step = from_columns(d_step) + d_logs * rate
-    d_dt_part = d_step * jax.nn.sigmoid(dt_in)
-    g_a_log = jnp.sum(d_logs * step, axis=0) * rate
+    d_xs, d_row, d_b, d_c = mix_back(
+        b_maps, c_maps, x_act, d_mixed, scanned, skip_row, row, head_width
+    )
+    d_logs = jnp.dot(d_row[:, per:].reshape(head_count, length), lower, precision=PRECISE)
+    d_step = d_row[:, :per].reshape(head_count, length) + d_logs * rate[:, None]
+    d_dt_part = (d_step * jax.nn.sigmoid(dt_in)).T
+    g_a_log = jnp.sum(d_logs * step, axis=1) * rate
     g_skip = jnp.sum((d_mixed * x_wide).reshape(length, head_count, head_width), axis=(0, 2))
 
     d_bc_part = jnp.concatenate([d_b, d_c], axis=1)

time: 220 us -> 211 us (0.959)
  Pallas kernels: 146 us -> 141 us
  local copies, waits for them, and re-layouts: 28.8 us -> 24.4 us
    pallas_call x1, Pallas kernels: 21 us -> 16.7 us  [mix_back(): pl.pallas_call(partial(back_kernel, per, width), grid=(groups,), in_specs...]
    reshape x8 -> x5, local copies, waits for them, and re-layouts: 3.66 us -> 0.2 us  [the longest x2 0.14 us: on_device(): d_step = d_row[:, :per].reshape(head_count, length) + d_logs * rate[:, None]]
    unnamed x75 -> x73, local copies, waits for them, and re-layouts: 9.14 us -> 9.13 us
where the time goes in v3:
time: 211 us; the launch traced here: 210 us
  Pallas kernels  141 us (67%)
  local copies, waits for them, and re-layouts  24.4 us (12%)
  other arithmetic  23.9 us (11%)
  matrix products  20.3 us (10%)
    pallas_call x1, Pallas kernels, closing(): pl.pallas_call(partial(closing_kernel, count, heads, tensors, side_at), o...  51.5 us
    pallas_call x1, Pallas kernels, ring_gather(): pl.pallas_call(partial(gather_kernel, count), out_shape=jax.ShapeDtypeStr...  46.3 us
    pallas_call x1, Pallas kernels, mix_back(): pl.pallas_call(partial(back_kernel, per, width), grid=(groups,), in_specs...  16.7 us
    pallas_call x2, Pallas kernels, group_sum(): pl.pallas_call(partial(group_sum_kernel, heads, tensors, scattered), out_...  14.8 us
    pallas_call x1, Pallas kernels, mix(): pl.pallas_call(partial(mix_kernel, per, width), grid=(inner // (per * wid...  11.3 us
    unnamed x73, local copies, waits for them, and re-layouts  9.13 us
    dot_general x3, matrix products, last_axes(): lax.dot_general(a, b, (((1,), (1,)), ((), ())), preferred_element_type=jn...  7.45 us
    dot_general x1, matrix products, on_device(): jnp.dot(cotangent, weight_out, preferred_element_type=jnp.float32)  4.49 us

profile of v3, /device:TPU:0, one launch (start us, length us, event | category | flops | bytes accessed | tf_op | source)
XLA Modules:
  0.0 210.5 jit_solution(15119604814272604544)
XLA Ops:
  0.6 1.0 copy.88
  1.7 1.0 copy.89
  2.7 0.9 bitcast_dynamic-update-slice_fusion.1
  4.4 1.0 copy.87
  6.2 46.3 %ring_gather.1 = bf16[8,128,1920]{2,1,0:T(8,128)(2,1)} custom-call(bf16[128,1920]{1,0:T(8,128)(2,1)} %copy-done.12), custom_call_target="tpu_custom_call" | custom-call | tf_op jit(solution)/shard_map/ring_gather/pallas_call | solution.py:87
  52.8 3.7 %fusion = f32[512,1408]{1,0:T(8,128)S(1)} fusion(bf16[1024,1920]{1,0:T(8,128)(2,1)} %bitcast.110, f32[1024]{0:T(1024)S(1)} %copy-done.25, f32[512]{0:T(512)S(1)} %add_rsqrt_fusion, bf16[512,1024]{1,0:T(8,128)(2,1)S(1)} %copy-done.4), kind=kOutput, calls=%fused_computation.2 | convolution fusion | flops 1478492160 | bytes 6821888 | tf_op jit(solution)/shard_map/dot_general | solution.py:658
  56.5 1.6 copy-done.3
  59.0 1.8 multiply_convert_fusion.3
  60.8 1.1 compare_select_fusion
  63.3 1.1 slice.278
  65.5 11.3 %mix.1.y_ref = f32[512,512]{1,0:T(8,128)} custom-call(bf16[512,128]{1,0:T(8,128)(2,1)} %get-tuple-element.118.b_ref, bf16[512,128]{1,0:T(8,128)(2,1)} %get-tuple-element.117.c_ref, bf16[512,512]{1,0:T(8,128)(2,1)} %get-tuple-element.109.x_ref, f32[4,8,512]{2,1,0:T(8,128)} %pad_maximum_fusion.6.row_ref), custom_call_target="tpu_custom_call" | custom-call | tf_op jit(solution)/shard_map/mix/pallas_call | solution.py:544
  77.0 4.5 %multiply_reduce_fusion.7 = (f32[512]{0:T(512)S(1)}, f32[512]{0:T(512)S(1)}, f32[512,512]{1,0:T(8,128)}, f32[512,512]{1,0:T(8,128)}) fusion(f32[512]{0:T(512)S(1)} %mul.435, f32[512,1408]{1,0:T(8,128)} %copy-done.3, f32[512,512]{1,0:T(8,128)} %mix.1.y_ref, bf16[512,512]{1,0:T(8,128)(2,1)S(1)} %copy-done.1, f32[512]{0:T(512)S(1)} %mul.429, ...), kind=kOutput, calls=%fused_computation.49 | convolution fusion | flops 540277760 | bytes 6823936 | tf_op jit(solution)/shard_map/dot_general | solution.py:686
  82.1 4.9 %group_sum_2.1 = f32[8,128]{1,0:T(8,128)} custom-call(f32[8,128]{1,0:T(8,128)} %pad_maximum_fusion.7.x_ref), custom_call_target="tpu_custom_call" | custom-call | tf_op jit(solution)/shard_map/group_sum_2/pallas_call | solution.py:417
  88.5 4.1 %fusion.18 = (f32[512]{0:T(512)S(1)}, f32[512,512]{1,0:T(8,128)}, bf16[512,512]{1,0:T(8,128)(2,1)}, f32[512]{0:T(512)S(1)}) fusion(bf16[512,512]{1,0:T(8,128)(2,1)S(1)} %copy-done.1, f32[512,1408]{1,0:T(8,128)} %copy-done.3, f32[512]{0:T(512)S(1)} %get-tuple-element.133, f32[512,512]{1,0:T(8,128)} %get-tuple-element.108, f32[512]{0:T(512)S(1)} %multiply_multiply_fusion.2, ...), kind=kLoop, calls=%fused_computation.35 | loop fusion | flops 6552576 | bytes 6305792 | tf_op jit(solution)/shard_map/reduce_sum | solution.py:706
  93.2 16.7 %mix_back.1 = (f32[512,512]{1,0:T(8,128)}, f32[4,8,512]{2,1,0:T(8,128)}, f32[512,128]{1,0:T(8,128)}, f32[512,128]{1,0:T(8,128)}) custom-call(bf16[512,128]{1,0:T(8,128)(2,1)} %get-tuple-element.118.b_ref, bf16[512,128]{1,0:T(8,128)(2,1)} %get-tuple-element.117.c_ref, bf16[512,512]{1,0:T(8,128)(2,1)} %get-tuple-element.109.x_ref, ...), custom_call_target="tpu_custom_call" | custom-call | tf_op jit(solution)/shard_map/mix_back/pallas_call | solution.py:560
  109.9 0.9 fusion.72
  111.1 1.7 fusion.54
  113.5 0.9 pad_maximum_fusion.1.x_ref
  114.4 9.9 %group_sum_5.1 = f32[512,128]{1,0:T(8,128)} custom-call(bf16[4,512,128]{2,1,0:T(8,128)(2,1)} %pad_maximum_fusion.1.x_ref), custom_call_target="tpu_custom_call" | custom-call | tf_op jit(solution)/shard_map/group_sum_5/pallas_call | solution.py:417
  124.5 1.3 multiply_reduce_fusion.12
  127.3 2.5 %multiply_reduce_fusion.5 = (f32[512]{0:T(512)S(1)}, f32[512]{0:T(512)S(1)}, f32[512]{0:T(512)S(1)}, f32[512]{0:T(512)S(1)}, f32[512,512]{1,0:T(8,128)S(1)}) fusion(f32[512,512]{1,0:T(8,128)S(1)} %slice.285, f32[512,1408]{1,0:T(8,128)} %copy-done.3, f32[512,512]{1,0:T(8,128)} %get-tuple-element.25, f32[512,512]{1,0:T(8,128)S(1)} %copy-done.7), kind=kLoop, calls=%fused_computation.43 | loop fusion | flops 4192256 | bytes 5251072 | tf_op jit(solution)/shard_map/reduce_sum | solution.py:610
  130.6 1.7 convolution_convert_fusion.1
  132.9 2.6 %fusion.2 = f32[512,1024]{1,0:T(8,128)} fusion(bf16[1024,1920]{1,0:T(8,128)(2,1)S(1)} %bitcast.114, bf16[512,512]{1,0:T(8,128)(2,1)S(1)} %copy-done.13, bf16[512,512]{1,0:T(8,128)(2,1)S(1)} %fusion.14), kind=kOutput, calls=%fused_computation.4 | convolution fusion | flops 1075838976 | bytes 5242880 | tf_op jit(solution)/shard_map/dot_general | solution.py:440
  136.1 1.1 slice_multiply_fusion
  137.2 3.1 %add_convert_fusion = bf16[512,1024]{1,0:T(8,128)(2,1)} fusion(f32[512,1024]{1,0:T(8,128)} %fusion.2, bf16[512,128]{1,0:T(8,128)(2,1)S(1)} %fusion.56, bf16[1024,16]{1,0:T(8,128)(2,1)S(1)} %slice_multiply_fusion, bf16[1024,64]{1,0:T(8,128)(2,1)S(1)} %constant_dynamic-slice_fusion.2), kind=kOutput, calls=%fused_computation.7 | convolution fusion | flops 136183808 | bytes 3440640 | tf_op jit(solution)/shard_map/dot_general | solution.py:440
  140.3 1.7 convolution_convert_fusion
  142.8 2.0 pad_maximum_fusion
  145.8 0.8 constant_dynamic-slice_fusion.1.feat_ref
  146.7 51.5 %closing.1 = (f32[128,1664]{1,0:T(8,128)}, bf16[4,128,1024]{2,1,0:T(8,128)(2,1)}, bf16[4,128,1024]{2,1,0:T(8,128)(2,1)}, f32[4,128,128]{2,1,0:T(8,128)}, f32[24,...) custom-call(bf16[8,128,1664]{2,1,0:T(8,128)(2,1)} %bitcast.109, bf16[4,128,1024]{2,1,0:T(8,128)(2,1)} %bitcast.116, ...), custom_call_target="tpu_custom_call" | custom-call | tf_op jit(solution)/shard_map/closing/pallas_call | solution.py:326
  198.2 3.0 %convert_add_fusion = f32[512,1024]{1,0:T(8,128)} fusion(bf16[512,1024]{1,0:T(8,128)(2,1)S(1)} %copy-done.8, bf16[4,128,1024]{2,1,0:T(8,128)(2,1)} %get-tuple-element.30), kind=kLoop, calls=%fused_computation.6 | loop fusion | flops 1572864 | bytes 4194304 | tf_op jit(solution)/shard_map/add | solution.py:777
  201.3 0.8 copy.101
  208.9 1.0 copy.124
  (151 shorter events, 21.7 us)
Async XLA Ops:
  5.4 0.8 copy-start.12
  6.2 46.3 %copy-start.4 = (bf16[512,1024]{1,0:T(8,128)(2,1)S(1)}, bf16[512,1024]{1,0:T(8,128)(2,1)}, u32[]{:S(2)}) copy-start(bf16[512,1024]{1,0:T(8,128)(2,1)} %param.14) | copy-start | bytes 3145732
  6.2 46.6 %copy-start.25 = (f32[1024]{0:T(1024)S(1)}, f32[1024]{0:T(1024)}, u32[]{:S(2)}) copy-start(f32[1024]{0:T(1024)} %param.16) | copy-start | bytes 12292
  56.5 1.6 copy-start.3
  58.1 0.8 copy-start.20
  58.1 2.7 %copy-start.27 = (f32[16]{0:T(128)S(1)}, f32[16]{0:T(128)}, u32[]{:S(2)}) copy-start(f32[16]{0:T(128)} %param.23) | copy-start | bytes 196
  58.9 3.0 %copy-start.29 = (f32[16]{0:T(128)S(1)}, f32[16]{0:T(128)}, u32[]{:S(2)}) copy-start(f32[16]{0:T(128)} %param.24) | copy-start | bytes 196
  59.0 5.4 %copy-start.22 = (f32[2,128,4]{1,2,0:T(4,128)S(1)}, f32[2,128,4]{1,2,0:T(4,128)}, u32[]{:S(2)}) copy-start(f32[2,128,4]{1,2,0:T(4,128)} %param.22) | copy-start | bytes 12292
  63.3 13.5 %copy-start.24 = (f32[16,32]{1,0:T(8,128)S(1)}, f32[16,32]{1,0:T(8,128)}, u32[]{:S(2)}) copy-start(f32[16,32]{1,0:T(8,128)} %param.26) | copy-start | bytes 6148
  63.3 13.6 %copy-start.28 = (f32[16]{0:T(128)S(1)}, f32[16]{0:T(128)}, u32[]{:S(2)}) copy-start(f32[16]{0:T(128)} %param.25) | copy-start | bytes 196
  63.3 13.7 %copy-start.1 = (bf16[512,512]{1,0:T(8,128)(2,1)S(1)}, bf16[512,512]{1,0:T(8,128)(2,1)}, u32[]{:S(2)}) copy-start(bf16[512,512]{1,0:T(8,128)(2,1)} %get-tuple-element.109.x_ref) | copy-start | bytes 1572868
  77.0 11.5 %copy-start = (f32[512,512]{1,0:T(8,128)S(1)}, f32[512,512]{1,0:T(8,128)}, u32[]{:S(2)}) copy-start(f32[512,512]{1,0:T(8,128)} %mix.1.y_ref) | copy-start | bytes 3145732
  109.9 2.8 %copy-start.18 = (f32[512,128]{1,0:T(8,128)S(1)}, f32[512,128]{1,0:T(8,128)}, u32[]{:S(2)}) copy-start(f32[512,128]{1,0:T(8,128)} %get-tuple-element.26) | copy-start | bytes 786436
  111.1 2.1 copy-start.17
  113.4 13.9 %copy-start.7 = (f32[512,512]{1,0:T(8,128)S(1)}, f32[512,512]{1,0:T(8,128)}, u32[]{:S(2)}) copy-start(f32[512,512]{1,0:T(8,128)} %get-tuple-element.110) | copy-start | bytes 3145732
  127.3 2.5 %copy-start.9 = (f32[512,128]{1,0:T(8,128)S(1)}, f32[512,128]{1,0:T(8,128)}, u32[]{:S(2)}) copy-start(f32[512,128]{1,0:T(8,128)} %group_sum_5.1) | copy-start | bytes 786436
  127.3 3.3 %copy-start.2 = (bf16[8,128,1920]{2,1,0:T(8,128)(2,1)S(1)}, bf16[8,128,1920]{2,1,0:T(8,128)(2,1)}, u32[]{:S(2)}) copy-start(bf16[8,128,1920]{2,1,0:T(8,128)(2,1)} %ring_gather.1) | copy-start | bytes 11796484
  127.3 3.3 %copy-start.6 = (f32[512,512]{1,0:T(8,128)S(1)}, f32[512,512]{1,0:T(8,128)}, u32[]{:S(2)}) copy-start(f32[512,512]{1,0:T(8,128)} %get-tuple-element.108) | copy-start | bytes 3145732
  130.6 2.2 %copy-start.13 = (bf16[512,512]{1,0:T(8,128)(2,1)S(1)}, bf16[512,512]{1,0:T(8,128)(2,1)}, u32[]{:S(2)}) copy-start(bf16[512,512]{1,0:T(8,128)(2,1)} %get-tuple-element.111) | copy-start | bytes 1572868
  132.8 2.6 %copy-start.15 = (bf16[512,512]{1,0:T(8,128)(2,1)}, bf16[512,512]{1,0:T(8,128)(2,1)S(1)}, u32[]{:S(2)}) copy-start(bf16[512,512]{1,0:T(8,128)(2,1)S(1)} %fusion.14) | copy-start | bytes 1572868
  136.0 4.2 %copy-start.5 = (bf16[512,1024]{1,0:T(8,128)(2,1)S(1)}, bf16[512,1024]{1,0:T(8,128)(2,1)}, u32[]{:S(2)}) copy-start(bf16[512,1024]{1,0:T(8,128)(2,1)} %param.14) | copy-start | bytes 3145732
  136.1 4.2 %copy-start.14 = (bf16[512,512]{1,0:T(8,128)(2,1)S(1)}, bf16[512,512]{1,0:T(8,128)(2,1)}, u32[]{:S(2)}) copy-start(bf16[512,512]{1,0:T(8,128)(2,1)} %get-tuple-element.111) | copy-start | bytes 1572868
  136.1 4.2 %copy-start.16 = (bf16[512,512]{1,0:T(8,128)(2,1)S(1)}, bf16[512,512]{1,0:T(8,128)(2,1)}, u32[]{:S(2)}) copy-start(bf16[512,512]{1,0:T(8,128)(2,1)} %copy-done.15) | copy-start | bytes 1572868
  140.3 1.7 copy-start.8
  198.2 3.0 %copy-start.11 = (f32[128,1664]{1,0:T(8,128)S(1)}, f32[128,1664]{1,0:T(8,128)}, u32[]{:S(2)}) copy-start(f32[128,1664]{1,0:T(8,128)} %get-tuple-element.32) | copy-start | bytes 2555908
  201.2 2.6 %copy-start.19 = (f32[4,128,128]{2,1,0:T(8,128)S(1)}, f32[4,128,128]{2,1,0:T(8,128)}, u32[]{:S(2)}) copy-start(f32[4,128,128]{2,1,0:T(8,128)} %get-tuple-element.33) | copy-start | bytes 786436
  201.2 3.5 %copy-start.21 = (f32[16,128]{1,0:T(8,128)S(1)}, f32[16,128]{1,0:T(8,128)}, u32[]{:S(2)}) copy-start(f32[16,128]{1,0:T(8,128)} %get-tuple-element.35) | copy-start | bytes 24580
  201.2 4.3 %copy-start.23 = (f32[24,128]{1,0:T(8,128)S(1)}, f32[24,128]{1,0:T(8,128)}, u32[]{:S(2)}) copy-start(f32[24,128]{1,0:T(8,128)} %get-tuple-element.34) | copy-start | bytes 36868
  201.3 7.6 %copy-start.10 = (bf16[4,128,1024]{2,1,0:T(8,128)(2,1)S(1)}, bf16[4,128,1024]{2,1,0:T(8,128)(2,1)}, u32[]{:S(2)}) copy-start(bf16[4,128,1024]{2,1,0:T(8,128)(2,1)} %get-tuple-element.29) | copy-start | bytes 3145732
  203.8 6.1 %copy-start.26 = (f32[1,1024]{1,0:T(1,128)S(1)}, f32[1,1024]{1,0:T(1,128)}, u32[]{:S(2)}) copy-start(f32[1,1024]{1,0:T(1,128)} %get-tuple-element.31) | copy-start | bytes 12292
